TPU v7x, 512 devices: a whole 4x4x16 slice. The times are simulated.
512 devices in a mesh: dp: 4 (over y), expert: 128 (over x, z, core).
Axes of the slice: x: 4, y: 4, z: 16, core: 2. Of those that a mesh axis runs over, the one named last changes fastest.
Arguments:
- tokens: bfloat16 [16384, 2048], P('expert', 'dp'), may hold values from -6 to 6
- routes: int32 [16384, 2], P('expert'), may hold values from 0 to 127, all different within a row; in each aligned block of 128 rows (0 to 127, 128 to 255, ...) at most 3 rows name the same one
- route_weights: float32 [16384, 2], P('expert'), may hold values from 0.02 to 0.3
- live_tokens: int32 [128], P('expert'), may hold values from 33 to 128, as said below
- gate_codes: bfloat16 [2048, 98304], P('dp', 'expert'), may hold values from -4 to 4
- gate_scales: float32 [16, 768], P('dp', 'expert'), may hold values from 0.011 to 0.044
- up_codes: bfloat16 [2048, 98304], P('dp', 'expert'), may hold values from -4 to 4
- up_scales: float32 [16, 768], P('dp', 'expert'), may hold values from 0.011 to 0.044
- down_codes: bfloat16 [98304, 2048], P('expert', 'dp'), may hold values from -4 to 4
- down_scales: float32 [768, 16], P('expert', 'dp'), may hold values from 0.018 to 0.072
- grad_out: bfloat16 [16384, 2048], P('expert', 'dp'), may hold values from -6 to 6
Outputs:
- grad_tokens: bfloat16 [16384, 2048], P('expert', 'dp')
- grad_route_weights: float32 [16384, 2], P('expert')
- grad_gate_proj: bfloat16 [2048, 98304], P('dp', 'expert')
- grad_up_proj: bfloat16 [2048, 98304], P('dp', 'expert')
- grad_down_proj: bfloat16 [98304, 2048], P('expert', 'dp')
Inputs may be any that keep to these rules, and one draw needn't show every extreme that they name: `routes`: in every aligned block of 128 rows (the tokens of one group) each row names 2 different experts, and no expert is named by more than 3 rows of the block; some expert is named by exactly 3 rows of some block. `live_tokens`: some group is full and some group holds the fewest live tokens.
All inputs are finite; a program needn't handle non-finite values.
Results may differ from a plain program's by a relative error of at most 0.023.
Values may be sent and summed in bfloat16 or wider, within the bound.
No kernel may reach another device: no remote copies, remote signals or barrier semaphores. Data moves between devices by JAX's collectives and lax.ppermute only.
A program may use at most 64 MiB of HBM per device.

v0:
```python
import jax
import jax.numpy as jnp
from jax import lax
from jax.sharding import PartitionSpec as P


def dequant(codes, scales):
    row_count, col_count = codes.shape
    block_size = row_count // scales.shape[0]
    blocks = codes.astype(jnp.float32).reshape(
        row_count // block_size, block_size, col_count // block_size, block_size
    )
    return (blocks * scales[:, None, :, None]).reshape(row_count, col_count).astype(jnp.bfloat16)


def activate(gate_pre, up_pre, grad_hidden):
    sigmoid_gate = jax.nn.sigmoid(gate_pre)
    activated = gate_pre * sigmoid_gate
    hidden = (activated * up_pre).astype(jnp.bfloat16)
    gate_delta = (
        grad_hidden * up_pre * sigmoid_gate * (1.0 + gate_pre * (1.0 - sigmoid_gate))
    ).astype(jnp.bfloat16)
    up_delta = (grad_hidden * activated).astype(jnp.bfloat16)
    return (hidden, gate_delta, up_delta)


def body(
    tokens,
    routes,
    route_weights,
    live_tokens,
    gate_codes,
    gate_scales,
    up_codes,
    up_scales,
    down_codes,
    down_scales,
    grad_out,
):
    tok_count, top_count = routes.shape
    experts = lax.axis_size("expert")
    quarter = tokens.shape[1]
    capacity = min(tok_count, max(2, 3 * tok_count * top_count // (2 * experts)))
    flat_count = tok_count * top_count
    slot_count = experts * capacity
    contract_last = (((1,), (1,)), ((), ()))
    contract_first = (((0,), (0,)), ((), ()))
    is_live = jnp.arange(tok_count, dtype=jnp.int32) < live_tokens[0]
    live_flat = jnp.repeat(is_live, top_count)
    expert_ids = routes.reshape(flat_count)
    one_hot = (
        (expert_ids[:, None] == jnp.arange(experts, dtype=jnp.int32)[None, :]) & live_flat[:, None]
    ).astype(jnp.int32)
    running = jnp.cumsum(one_hot, axis=0)
    position = jnp.sum(one_hot * running, axis=1) - 1
    slot_index = jnp.where(live_flat, expert_ids * capacity + position, slot_count)
    weight_flat = jnp.where(live_flat, route_weights.reshape(flat_count), 0.0)
    scaled = (
        weight_flat[:, None] * jnp.repeat(grad_out, top_count, axis=0).astype(jnp.float32)
    ).astype(jnp.bfloat16)
    send_rows = (
        jnp.zeros((slot_count, quarter), jnp.bfloat16)
        .at[slot_index]
        .set(jnp.repeat(tokens, top_count, axis=0), mode="drop")
    )
    send_grads = (
        jnp.zeros((slot_count, quarter), jnp.bfloat16).at[slot_index].set(scaled, mode="drop")
    )
    arrived, arrived_grads = (
        lax.all_to_all(
            send_rows.reshape(experts, capacity, quarter),
            "expert",
            split_axis=0,
            concat_axis=0,
            tiled=True,
        ),
        lax.all_to_all(
            send_grads.reshape(experts, capacity, quarter),
            "expert",
            split_axis=0,
            concat_axis=0,
            tiled=True,
        ),
    )
    token_rows = arrived.reshape(slot_count, quarter)
    scaled_rows = arrived_grads.reshape(slot_count, quarter)
    w_gate = dequant(gate_codes, gate_scales)
    w_up = dequant(up_codes, up_scales)
    w_down = dequant(down_codes, down_scales)
    gate_part = jnp.dot(token_rows, w_gate, preferred_element_type=jnp.float32).astype(jnp.bfloat16)
    up_part = jnp.dot(token_rows, w_up, preferred_element_type=jnp.float32).astype(jnp.bfloat16)
    back_part = lax.dot_general(
        scaled_rows, w_down, contract_last, preferred_element_type=jnp.float32
    ).astype(jnp.bfloat16)
    gate_pre, up_pre, grad_hidden = (
        lax.psum(gate_part, "dp").astype(jnp.float32),
        lax.psum(up_part, "dp").astype(jnp.float32),
        lax.psum(back_part, "dp").astype(jnp.float32),
    )
    hidden, gate_delta, up_delta = activate(gate_pre, up_pre, grad_hidden)
    expert_out = (
        jnp.dot(hidden, w_down, preferred_element_type=jnp.float32)
        .astype(jnp.bfloat16)
        .reshape(experts, capacity, quarter)
    )
    grad_rows = (
        (
            lax.dot_general(gate_delta, w_gate, contract_last, preferred_element_type=jnp.float32)
            + lax.dot_general(up_delta, w_up, contract_last, preferred_element_type=jnp.float32)
        )
        .astype(jnp.bfloat16)
        .reshape(experts, capacity, quarter)
    )
    grad_gate_proj = lax.dot_general(
        token_rows, gate_delta, contract_first, preferred_element_type=jnp.float32
    ).astype(jnp.bfloat16)
    grad_up_proj = lax.dot_general(
        token_rows, up_delta, contract_first, preferred_element_type=jnp.float32
    ).astype(jnp.bfloat16)
    grad_down_proj = lax.dot_general(
        hidden, scaled_rows, contract_first, preferred_element_type=jnp.float32
    ).astype(jnp.bfloat16)
    returned = lax.all_to_all(expert_out, "expert", split_axis=0, concat_axis=0, tiled=True)
    returned_grads = lax.all_to_all(grad_rows, "expert", split_axis=0, concat_axis=0, tiled=True)
    safe_slot = jnp.minimum(slot_index, slot_count - 1)
    zero_bf = jnp.zeros((), jnp.bfloat16)
    routed_out = jnp.where(
        live_flat[:, None], returned.reshape(slot_count, quarter)[safe_slot], zero_bf
    )
    routed_grad = jnp.where(
        live_flat[:, None], returned_grads.reshape(slot_count, quarter)[safe_slot], zero_bf
    )
    routed_out = routed_out.reshape(tok_count, top_count, quarter).astype(jnp.float32)
    grad_tokens = jnp.sum(
        routed_grad.reshape(tok_count, top_count, quarter).astype(jnp.float32), axis=1
    ).astype(jnp.bfloat16)
    gate_terms = jnp.einsum("td,tkd->tk", grad_out.astype(jnp.float32), routed_out)
    grad_route_weights = lax.psum(gate_terms, "dp")
    return (grad_tokens, grad_route_weights, grad_gate_proj, grad_up_proj, grad_down_proj)


def solution(mesh):
    placed = (
        P("expert", "dp"),
        P("expert", None),
        P("expert", None),
        P("expert"),
        P("dp", "expert"),
        P("dp", "expert"),
        P("dp", "expert"),
        P("dp", "expert"),
        P("expert", "dp"),
        P("expert", "dp"),
        P("expert", "dp"),
    )
    return jax.shard_map(
        body,
        mesh=mesh,
        in_specs=placed,
        out_specs=(
            P("expert", "dp"),
            P("expert", None),
            P("dp", "expert"),
            P("dp", "expert"),
            P("expert", "dp"),
        ),
        check_vma=False,
    )
```

profile of v0, /device:TPU:1, one launch (start us, length us, event | category | flops | bytes accessed | tf_op | source)
XLA Modules:
  0.0 278.9 jit_solution(6609425183401745266)
XLA Ops:
  7.2 0.8 copy.18
  9.3 0.7 broadcast_multiply_fusion
  10.5 0.3 fusion.21
  11.0 0.2 fusion.22
  11.8 1.6 scatter_custom_fusion.1
  13.4 1.0 reshape.180
  14.4 20.4 %all-to-all-start.1 = ((bf16[128,3,512]{2,1,0:T(4,128)(2,1)}), bf16[128,3,512]{2,1,0:T(4,128)(2,1)S(1)}, u32[]{:S(2)}, u32[]{:S(2)}) async-start(bf16[128,3,512]{2,1,0:T(4,128)(2,1)} %reshape.180), calls=%async_computation.1 | async-start | bytes 1048576 | tf_op jit(solution)/shard_map/all_to_all | solution.py:70
  35.2 0.4 convert_element_type.81
  35.6 1.7 scatter_custom_fusion
  37.3 1.0 reshape.177
  38.3 29.7 %all-to-all-done.1 = bf16[128,3,512]{2,1,0:T(4,128)(2,1)S(1)} async-done(((bf16[128,3,512]{2,1,0:T(4,128)(2,1)}), bf16[128,3,512]{2,1,0:T(4,128)(2,1)S(1)}, u32[]{:S(2)}, u32[]{:S(2)}) %all-to-all-start.1) | async-done | bytes 393248 | tf_op jit(solution)/shard_map/all_to_all | solution.py:70
  68.0 7.6 %all-to-all-start = ((bf16[128,3,512]{2,1,0:T(4,128)(2,1)}), bf16[128,3,512]{2,1,0:T(4,128)(2,1)}, u32[]{:S(2)}, u32[]{:S(2)}) async-start(bf16[128,3,512]{2,1,0:T(4,128)(2,1)} %reshape.177), calls=%async_computation | async-start | bytes 1048576 | tf_op jit(solution)/shard_map/all_to_all | solution.py:77
  75.6 0.2 all-reduce.3.cloned.1.call-start
  76.0 0.3 copy.27
  76.4 1.4 copy.25
  77.8 0.3 reshape.181
  78.2 0.3 mul.98
  78.5 1.4 convolution_convert_fusion.3
  79.8 0.3 mul.94
  80.1 1.2 copy-done
  81.3 1.3 convolution_convert_fusion.4
  82.6 25.9 %all-to-all-done = bf16[128,3,512]{2,1,0:T(4,128)(2,1)} async-done(((bf16[128,3,512]{2,1,0:T(4,128)(2,1)}), bf16[128,3,512]{2,1,0:T(4,128)(2,1)}, u32[]{:S(2)}, u32[]{:S(2)}) %all-to-all-start) | async-done | bytes 393248 | tf_op jit(solution)/shard_map/all_to_all | solution.py:77
  108.4 1.4 reshape.178
  109.9 0.3 mul.91
  110.1 1.1 copy-done.2
  111.3 1.3 convolution_convert_fusion.5
  112.7 60.9 %all-reduce.3.cloned.1.call-done = (bf16[384,768]{1,0:T(8,128)(2,1)}, bf16[384,768]{1,0:T(8,128)(2,1)}, bf16[384,768]{1,0:T(8,128)(2,1)}) async-done(((bf16[384,768]{1,0:T(8,128)(2,1)}, bf16[384,768]{1,0:T(8,128)(2,1)}, bf16[384,768]{1,0:T(8,128)(2,1)}), (bf16[384,768]{1,0:T(8,128)(2,1)}, bf16[384,768]{1,0:T(8,128)(2,1)}, bf16[384,768]{1,0:T(8,128)(2,1)})) %all-reduce.3.cloned.1.call-update) | async-done | bytes 1769488 | tf_op jit(solution)/shard_map/psum | solution.py:97
  173.5 3.1 %convolution_convert_fusion.6 = bf16[384,512]{1,0:T(8,128)(2,1)} fusion(f32[96,8,4,128]{3,2,1,0:T(4,128)} %bitcast.60, bf16[768,512]{1,0:T(8,128)(2,1)S(1)} %copy-done.9, bf16[384,768]{1,0:T(8,128)(2,1)} %get-tuple-element.5, bf16[384,768]{1,0:T(8,128)(2,1)} %get-tuple-element.7), kind=kOutput, calls=%fused_computation.24 | convolution fusion | flops 305725440 | bytes 3932160 | tf_op jit(solution)/shard_map/dot_general | solution.py:102
  176.7 2.1 reshape.184
  178.7 17.3 %all-to-all-start.3 = ((bf16[128,3,512]{2,1,0:T(4,128)(2,1)}), bf16[128,3,512]{2,1,0:T(4,128)(2,1)}, u32[]{:S(2)}, u32[]{:S(2)}) async-start(bf16[128,3,512]{2,1,0:T(4,128)(2,1)} %reshape.184), calls=%async_computation.3 | async-start | bytes 1048576 | tf_op jit(solution)/shard_map/all_to_all | solution.py:123
  196.0 2.0 fusion.7
  198.0 0.5 fusion.33
  198.5 0.9 copy-done.1
  199.9 0.6 fusion.3
  200.5 1.0 reshape.182
  201.6 27.3 %all-to-all-done.3 = bf16[128,3,512]{2,1,0:T(4,128)(2,1)} async-done(((bf16[128,3,512]{2,1,0:T(4,128)(2,1)}), bf16[128,3,512]{2,1,0:T(4,128)(2,1)}, u32[]{:S(2)}, u32[]{:S(2)}) %all-to-all-start.3) | async-done | bytes 393248 | tf_op jit(solution)/shard_map/all_to_all | solution.py:123
  228.9 7.1 %all-to-all-start.2 = ((bf16[128,3,512]{2,1,0:T(4,128)(2,1)}), bf16[128,3,512]{2,1,0:T(4,128)(2,1)S(1)}, u32[]{:S(2)}, u32[]{:S(2)}) async-start(bf16[128,3,512]{2,1,0:T(4,128)(2,1)} %reshape.182), calls=%async_computation.2 | async-start | bytes 1048576 | tf_op jit(solution)/shard_map/all_to_all | solution.py:124
  236.0 1.5 convolution_convert_fusion.2
  237.5 1.6 convolution_convert_fusion.1
  239.1 1.5 convolution_convert_fusion
  240.7 1.4 reshape.185
  242.1 1.2 gather_fusion.1
  243.4 0.8 fusion.16
  244.2 8.1 %psum.31 = f32[128,2]{0,1:T(2,128)} all-reduce(f32[128,2]{0,1:T(2,128)S(1)} %bitcast.65), channel_id=1, replica_groups=mesh['dp'=4,'expert'=128] {'dp'}, use_global_device_ids=true, to_apply=%region_9.10 | all-reduce | flops 256 | bytes 2048 | tf_op jit(solution)/shard_map/psum | solution.py:138
  252.4 16.8 %all-to-all-done.2 = bf16[128,3,512]{2,1,0:T(4,128)(2,1)S(1)} async-done(((bf16[128,3,512]{2,1,0:T(4,128)(2,1)}), bf16[128,3,512]{2,1,0:T(4,128)(2,1)S(1)}, u32[]{:S(2)}, u32[]{:S(2)}) %all-to-all-start.2) | async-done | bytes 393248 | tf_op jit(solution)/shard_map/all_to_all | solution.py:124
  269.2 0.3 reshape.183
  269.5 1.2 gather_fusion
  270.8 1.3 fusion.15
  (80 shorter events, 3.4 us)
Async XLA Ops:
  7.2 4.3 %copy-start.15 = (bf16[128,512]{1,0:T(8,128)(2,1)S(1)}, bf16[128,512]{1,0:T(8,128)(2,1)}, u32[]{:S(2)}) copy-start(bf16[128,512]{1,0:T(8,128)(2,1)} %param.11) | copy-start | bytes 393220
  8.9 1.2 copy-start.18
  11.8 23.0 %copy-start.23 = (f32[128,2]{0,1:T(2,128)S(1)}, f32[128,2]{0,1:T(2,128)}, u32[]{:S(2)}) copy-start(f32[128,2]{0,1:T(2,128)} %param.13) | copy-start | bytes 3076
  11.8 23.3 %copy-start.16 = (bf16[128,512]{1,0:T(8,128)(2,1)S(1)}, bf16[128,512]{1,0:T(8,128)(2,1)}, u32[]{:S(2)}) copy-start(bf16[128,512]{1,0:T(8,128)(2,1)} %param.21) | copy-start | bytes 393220
  14.4 53.6 %all-to-all-start.1 = ((bf16[128,3,512]{2,1,0:T(4,128)(2,1)}), bf16[128,3,512]{2,1,0:T(4,128)(2,1)S(1)}, u32[]{:S(2)}, u32[]{:S(2)}) async-start(bf16[128,3,512]{2,1,0:T(4,128)(2,1)} %reshape.180), calls=%async_computation.1 | async-start | bytes 1048576 | tf_op jit(solution)/shard_map/all_to_all | solution.py:70
  37.3 38.6 %copy-start.20 = (f32[6,4]{0,1:T(4,128)S(1)}, f32[6,4]{0,1:T(4,128)}, u32[]{:S(2)}) copy-start(f32[6,4]{0,1:T(4,128)} %param.20) | copy-start | bytes 292
  37.3 38.6 %copy-start.21 = (f32[4,6]{1,0:T(4,128)S(1)}, f32[4,6]{1,0:T(4,128)}, u32[]{:S(2)}) copy-start(f32[4,6]{1,0:T(4,128)} %param.16) | copy-start | bytes 292
  37.3 38.7 %copy-start.7 = (bf16[512,768]{1,0:T(8,128)(2,1)S(1)}, bf16[512,768]{1,0:T(8,128)(2,1)}, u32[]{:S(2)}) copy-start(bf16[512,768]{1,0:T(8,128)(2,1)} %param.15) | copy-start | bytes 2359300
  38.3 38.0 %copy-start.22 = (f32[4,6]{1,0:T(4,128)S(1)}, f32[4,6]{1,0:T(4,128)}, u32[]{:S(2)}) copy-start(f32[4,6]{1,0:T(4,128)} %param.18) | copy-start | bytes 292
  68.0 40.5 %all-to-all-start = ((bf16[128,3,512]{2,1,0:T(4,128)(2,1)}), bf16[128,3,512]{2,1,0:T(4,128)(2,1)}, u32[]{:S(2)}, u32[]{:S(2)}) async-start(bf16[128,3,512]{2,1,0:T(4,128)(2,1)} %reshape.177), calls=%async_computation | async-start | bytes 1048576 | tf_op jit(solution)/shard_map/all_to_all | solution.py:77
  75.6 97.9 %all-reduce.3.cloned.1.call-start = ((), (), s32[]{:S(2)}) async-start(), calls=%async_computation.4 | async-start | bytes 3538944 | tf_op jit(solution)/shard_map/psum | solution.py:97
  77.8 2.3 copy-start.3
  80.1 1.2 copy-start
  109.8 2.8 %copy-start.5 = (bf16[384,512]{1,0:T(8,128)(2,1)}, bf16[384,512]{1,0:T(8,128)(2,1)S(1)}, u32[]{:S(2)}) copy-start(bf16[384,512]{1,0:T(8,128)(2,1)S(1)} %reshape.178) | copy-start | bytes 1179652
  109.8 1.5 copy-start.8
  110.1 1.1 copy-start.2
  112.7 60.9 %copy-start.9 = (bf16[768,512]{1,0:T(8,128)(2,1)S(1)}, bf16[768,512]{1,0:T(8,128)(2,1)}, u32[]{:S(2)}) copy-start(bf16[768,512]{1,0:T(8,128)(2,1)} %param.19) | copy-start | bytes 2359300
  178.7 50.1 %all-to-all-start.3 = ((bf16[128,3,512]{2,1,0:T(4,128)(2,1)}), bf16[128,3,512]{2,1,0:T(4,128)(2,1)}, u32[]{:S(2)}, u32[]{:S(2)}) async-start(bf16[128,3,512]{2,1,0:T(4,128)(2,1)} %reshape.184), calls=%async_computation.3 | async-start | bytes 1048576 | tf_op jit(solution)/shard_map/all_to_all | solution.py:123
  198.0 1.4 copy-start.1
  198.0 1.6 copy-start.4
  198.0 1.8 copy-start.11
  198.0 1.9 copy-start.13
  201.6 35.9 %copy-start.12 = (bf16[384,768]{1,0:T(8,128)(2,1)S(1)}, bf16[384,768]{1,0:T(8,128)(2,1)}, u32[]{:S(2)}) copy-start(bf16[384,768]{1,0:T(8,128)(2,1)} %get-tuple-element.7) | copy-start | bytes 1769476
  201.6 35.9 %copy-start.14 = (bf16[384,768]{1,0:T(8,128)(2,1)S(1)}, bf16[384,768]{1,0:T(8,128)(2,1)}, u32[]{:S(2)}) copy-start(bf16[384,768]{1,0:T(8,128)(2,1)} %get-tuple-element.6) | copy-start | bytes 1769476
  228.9 40.3 %all-to-all-start.2 = ((bf16[128,3,512]{2,1,0:T(4,128)(2,1)}), bf16[128,3,512]{2,1,0:T(4,128)(2,1)S(1)}, u32[]{:S(2)}, u32[]{:S(2)}) async-start(bf16[128,3,512]{2,1,0:T(4,128)(2,1)} %reshape.182), calls=%async_computation.2 | async-start | bytes 1048576 | tf_op jit(solution)/shard_map/all_to_all | solution.py:124
  237.5 1.6 copy-start.6
  237.5 1.6 copy-start.10
  242.1 1.3 copy-start.17
  242.1 1.3 copy-start.19
Sparse Core Ops, SparseCore 0:
  112.8 60.6 all-reduce.2
where the time goes:
time: 280 us; the launch traced here: 279 us
  waiting for transfers between devices  161 us (58%)
  starting transfers between devices  52.6 us (19%)
  local copies, waits for them, and re-layouts  22.6 us (8%)
  between operations  15.2 us (5%)
  matrix products  13.7 us (5%)
  blocking collectives  8.13 us (3%)
  other arithmetic  6.24 us (2%)
    psum x1, waiting for transfers between devices, body(): lax.psum(up_part, 'dp').astype(jnp.float32)  60.9 us
    all_to_all x1, waiting for transfers between devices, body(): lax.all_to_all(send_rows.reshape(experts, capacity, quarter), 'expert', s...  29.7 us
    all_to_all x1, waiting for transfers between devices, body(): lax.all_to_all(expert_out, 'expert', split_axis=0, concat_axis=0, tiled=T...  27.3 us
    all_to_all x1, waiting for transfers between devices, body(): lax.all_to_all(send_grads.reshape(experts, capacity, quarter), 'expert',...  25.9 us
    all_to_all x1, starting transfers between devices, body(): lax.all_to_all(send_rows.reshape(experts, capacity, quarter), 'expert', s...  20.4 us
    all_to_all x1, starting transfers between devices, body(): lax.all_to_all(expert_out, 'expert', split_axis=0, concat_axis=0, tiled=T...  17.3 us
    all_to_all x1, waiting for transfers between devices, body(): lax.all_to_all(grad_rows, 'expert', split_axis=0, concat_axis=0, tiled=True)  16.8 us
    psum x1, blocking collectives, body(): grad_route_weights = lax.psum(gate_terms, 'dp')  8.13 us
  transfers between devices with their start and end apart: 5, of which 5 were waited for; matrix products, arithmetic and copies ran while one was open for 8% of the time, Pallas kernels for 0%

commit v1 on v0

v1 whole, which is shorter than its diff:
```python
import jax
import jax.numpy as jnp
from jax import lax
from jax.experimental import pallas as pl
from jax.experimental.pallas import tpu as pltpu
from jax.sharding import PartitionSpec as P

BF = jnp.bfloat16
F32 = jnp.float32
CAP = 3
QPAD = 16
LAST = (((1,), (1,)), ((), ()))
FIRST = (((0,), (0,)), ((), ()))
VMEM = pl.BlockSpec(memory_space=pltpu.VMEM)
SMEM = pl.BlockSpec(memory_space=pltpu.SMEM)


def split3(v):
    hi = v.astype(BF)
    rest = v - hi.astype(F32)
    mid = rest.astype(BF)
    lo = (rest - mid.astype(F32)).astype(BF)
    return hi, mid, lo


def call(kernel, outs, in_specs, args, flops=0, nbytes=0, scratch=()):
    return pl.pallas_call(
        kernel,
        out_shape=outs,
        in_specs=in_specs,
        out_specs=jax.tree.map(lambda _: VMEM, outs),
        scratch_shapes=scratch,
        cost_estimate=pl.CostEstimate(flops=flops, bytes_accessed=nbytes, transcendentals=0),
    )(*args)


def slot_kernel(live_ref, routes_ref, weights_ref, tokens_ref, grad_ref, send_ref, slots_ref):
    slots, count = slots_ref.shape
    quarter = tokens_ref.shape[1]
    row = lax.broadcasted_iota(jnp.int32, (slots, count), 0)
    token = lax.broadcasted_iota(jnp.int32, (slots, count), 1)
    expert = row // CAP
    live = token < live_ref[0]
    first = (routes_ref[0:1, :] == expert) & live
    second = (routes_ref[1:2, :] == expert) & live
    member = first | second
    before = (
        lax.broadcasted_iota(jnp.int32, (count, count), 0)
        < lax.broadcasted_iota(jnp.int32, (count, count), 1)
    ).astype(BF)
    ahead = jnp.dot(member.astype(BF), before, preferred_element_type=F32)
    chosen = member & (ahead == (row - expert * CAP).astype(F32))
    one_hot = chosen.astype(BF)
    slots_ref[...] = one_hot
    send_ref[:, :quarter] = jnp.dot(
        one_hot, tokens_ref[...], preferred_element_type=F32
    ).astype(BF)
    weight = jnp.where(first, weights_ref[0:1, :], weights_ref[1:2, :])
    weight = jnp.where(chosen, weight, 0.0)
    total = jnp.zeros((slots, quarter), F32)
    for piece in split3(weight):
        total = total + jnp.dot(piece, grad_ref[...], preferred_element_type=F32)
    send_ref[:, quarter:] = total.astype(BF)


def dequant_kernel(gs_ref, us_ref, ds_ref, gc_ref, uc_ref, dc_ref, wg_ref, wu_ref, wd_ref):
    for scale_ref, code_ref, out_ref in (
        (gs_ref, gc_ref, wg_ref),
        (us_ref, uc_ref, wu_ref),
        (ds_ref, dc_ref, wd_ref),
    ):
        for i in range(scale_ref.shape[0]):
            for j in range(scale_ref.shape[1]):
                block = (slice(i * 128, i * 128 + 128), slice(j * 128, j * 128 + 128))
                out_ref[block] = (code_ref[block].astype(F32) * scale_ref[i, j]).astype(BF)


def partial_kernel(rows_ref, wg_ref, wu_ref, wd_ref, out_ref):
    parts = out_ref.shape[0]
    quarter = wg_ref.shape[0]
    span = out_ref.shape[1] // 3
    gate = jnp.dot(rows_ref[:, :quarter], wg_ref[...], preferred_element_type=F32).astype(BF)
    for j in range(parts):
        out_ref[j, 0:span, :] = gate[j * span : (j + 1) * span]
    up = jnp.dot(rows_ref[:, :quarter], wu_ref[...], preferred_element_type=F32).astype(BF)
    for j in range(parts):
        out_ref[j, span : 2 * span, :] = up[j * span : (j + 1) * span]
    back = lax.dot_general(
        rows_ref[:, quarter:], wd_ref[...], LAST, preferred_element_type=F32
    ).astype(BF)
    for j in range(parts):
        out_ref[j, 2 * span : 3 * span, :] = back[j * span : (j + 1) * span]


def act_kernel(part_ref, out_ref):
    parts = part_ref.shape[0]
    span = part_ref.shape[1] // 3

    def total(k):
        lines = slice(k * span, (k + 1) * span)
        acc = part_ref[0, lines, :].astype(F32)
        for j in range(1, parts):
            acc = acc + part_ref[j, lines, :].astype(F32)
        return acc

    gate_pre, up_pre, grad_hidden = total(0), total(1), total(2)
    sig = jax.nn.sigmoid(gate_pre)
    activated = gate_pre * sig
    hidden = (activated * up_pre).astype(BF)
    gate_delta = (grad_hidden * up_pre * sig * (1.0 + gate_pre * (1.0 - sig))).astype(BF)
    up_delta = (grad_hidden * activated).astype(BF)
    prod = hidden.astype(F32) * grad_hidden
    prod = jnp.concatenate([prod, jnp.zeros((128 - span, prod.shape[1]), F32)], axis=0)
    ones = jnp.ones((QPAD, prod.shape[1]), BF)
    score = jnp.zeros((QPAD, 128), F32)
    for piece in split3(prod):
        score = score + lax.dot_general(ones, piece, LAST, preferred_element_type=F32)
    hi, mid, lo = split3(score)
    line = lax.broadcasted_iota(jnp.int32, (QPAD, 128), 0)
    scores = jnp.where(
        line == 0,
        hi.astype(F32),
        jnp.where(line == 1, mid.astype(F32), jnp.where(line == 2, lo.astype(F32), 0.0)),
    ).astype(BF)
    for j in range(parts):
        out_ref[j, 0:span, :] = gate_delta
        out_ref[j, span : 2 * span, :] = up_delta
        out_ref[j, 2 * span : 3 * span, :] = hidden
        out_ref[j, 3 * span : 3 * span + QPAD, 0:128] = scores


def back_kernel(act_ref, wg_ref, wu_ref, out_ref):
    parts = act_ref.shape[0]
    span = (act_ref.shape[1] - QPAD) // 3
    quarter = wg_ref.shape[0]
    eye = (
        lax.broadcasted_iota(jnp.int32, (span, 128), 0)
        == lax.broadcasted_iota(jnp.int32, (span, 128), 1)
    ).astype(BF)
    gate_delta = jnp.concatenate([act_ref[j, 0:span, :] for j in range(parts)], axis=0)
    up_delta = jnp.concatenate([act_ref[j, span : 2 * span, :] for j in range(parts)], axis=0)
    grad = lax.dot_general(gate_delta, wg_ref[...], LAST, preferred_element_type=F32)
    grad = grad + lax.dot_general(up_delta, wu_ref[...], LAST, preferred_element_type=F32)
    out_ref[:, :quarter] = grad.astype(BF)
    for j in range(parts):
        scores = act_ref[j, 3 * span : 3 * span + QPAD, 0:128]
        scores = jnp.concatenate([scores, jnp.zeros((128 - QPAD, 128), BF)], axis=0)
        out_ref[j * span : (j + 1) * span, quarter:] = lax.dot_general(
            eye, scores, LAST, preferred_element_type=F32
        ).astype(BF)


def weight_grad_kernel(rows_ref, act_ref, gg_ref, gu_ref, gd_ref):
    parts = act_ref.shape[0]
    span = (act_ref.shape[1] - QPAD) // 3
    quarter = gg_ref.shape[0]

    def gathered(k):
        return jnp.concatenate(
            [act_ref[j, k * span : (k + 1) * span, :] for j in range(parts)], axis=0
        )

    gg_ref[...] = lax.dot_general(
        rows_ref[:, :quarter], gathered(0), FIRST, preferred_element_type=F32
    ).astype(BF)
    gu_ref[...] = lax.dot_general(
        rows_ref[:, :quarter], gathered(1), FIRST, preferred_element_type=F32
    ).astype(BF)
    gd_ref[...] = lax.dot_general(
        gathered(2), rows_ref[:, quarter:], FIRST, preferred_element_type=F32
    ).astype(BF)


def home_kernel(routes_ref, weights_ref, slots_ref, ret_ref, grad_ref, score_ref):
    slots, count = slots_ref.shape
    quarter = grad_ref.shape[1]
    one_hot = slots_ref[...]
    grad_ref[...] = lax.dot_general(
        one_hot, ret_ref[:, :quarter], FIRST, preferred_element_type=F32
    ).astype(BF)
    pieces = ret_ref[:, quarter:].astype(F32)
    score = pieces[:, 0:1] + pieces[:, 1:2] + pieces[:, 2:3]
    picked = one_hot.astype(F32) * score
    expert = lax.broadcasted_iota(jnp.int32, (slots, count), 0) // CAP
    for k in range(2):
        mine = jnp.where(routes_ref[k : k + 1, :] == expert, picked, 0.0)
        score_ref[k : k + 1, :] = jnp.sum(mine, axis=0, keepdims=True) / weights_ref[k : k + 1, :]


def body(
    tokens,
    routes,
    route_weights,
    live_tokens,
    gate_codes,
    gate_scales,
    up_codes,
    up_scales,
    down_codes,
    down_scales,
    grad_out,
):
    count, quarter = tokens.shape
    hidden_size = gate_codes.shape[1]
    experts = lax.axis_size("expert")
    parts = lax.axis_size("dp")
    slots = experts * CAP
    span = slots // parts
    shape = jax.ShapeDtypeStruct
    routes_t = routes.T
    weights_t = route_weights.T

    send, one_hot = call(
        slot_kernel,
        (shape((slots, 2 * quarter), BF), shape((slots, count), BF)),
        [SMEM, VMEM, VMEM, VMEM, VMEM],
        (live_tokens, routes_t, weights_t, tokens, grad_out),
        flops=2 * slots * count * quarter * 4,
        nbytes=2 * slots * 2 * quarter,
    )
    arrived = lax.all_to_all(
        send.reshape(experts, CAP, 2 * quarter), "expert", split_axis=0, concat_axis=0, tiled=True
    )
    w_gate, w_up, w_down = call(
        dequant_kernel,
        (
            shape(gate_codes.shape, BF),
            shape(up_codes.shape, BF),
            shape(down_codes.shape, BF),
        ),
        [SMEM] * 3 + [VMEM] * 3,
        (gate_scales, up_scales, down_scales, gate_codes, up_codes, down_codes),
        flops=3 * quarter * hidden_size,
        nbytes=12 * quarter * hidden_size,
    )
    rows = arrived.reshape(slots, 2 * quarter)
    part = call(
        partial_kernel,
        shape((parts, 3 * span, hidden_size), BF),
        [VMEM] * 4,
        (rows, w_gate, w_up, w_down),
        flops=6 * slots * quarter * hidden_size,
        nbytes=8 * slots * hidden_size,
    )
    part = lax.all_to_all(part, "dp", split_axis=0, concat_axis=0, tiled=True)
    act = call(
        act_kernel,
        shape((parts, 3 * span + QPAD, hidden_size), BF),
        [VMEM],
        (part,),
        flops=60 * span * hidden_size,
        nbytes=16 * slots * hidden_size,
    )
    act = lax.all_to_all(act, "dp", split_axis=0, concat_axis=0, tiled=True)
    ret = call(
        back_kernel,
        shape((slots, quarter + 128), BF),
        [VMEM] * 3,
        (act, w_gate, w_up),
        flops=4 * slots * quarter * hidden_size,
        nbytes=8 * slots * hidden_size,
    )
    ret = lax.all_to_all(
        ret.reshape(experts, CAP, quarter + 128), "expert", split_axis=0, concat_axis=0, tiled=True
    )
    grad_gate, grad_up, grad_down = call(
        weight_grad_kernel,
        (
            shape((quarter, hidden_size), BF),
            shape((quarter, hidden_size), BF),
            shape((hidden_size, quarter), BF),
        ),
        [VMEM] * 2,
        (rows, act),
        flops=6 * slots * quarter * hidden_size,
        nbytes=16 * slots * hidden_size,
    )
    grad_tokens, grad_weights_t = call(
        home_kernel,
        (shape((count, quarter), BF), shape((2, count), F32)),
        [VMEM] * 4,
        (routes_t, weights_t, one_hot, ret.reshape(slots, quarter + 128)),
        flops=2 * slots * count * quarter,
        nbytes=2 * slots * quarter,
    )
    return (grad_tokens, grad_weights_t.T, grad_gate, grad_up, grad_down)


def solution(mesh):
    placed = (
        P("expert", "dp"),
        P("expert", None),
        P("expert", None),
        P("expert"),
        P("dp", "expert"),
        P("dp", "expert"),
        P("dp", "expert"),
        P("dp", "expert"),
        P("expert", "dp"),
        P("expert", "dp"),
        P("expert", "dp"),
    )
    return jax.shard_map(
        body,
        mesh=mesh,
        in_specs=placed,
        out_specs=(
            P("expert", "dp"),
            P("expert", None),
            P("dp", "expert"),
            P("dp", "expert"),
            P("expert", "dp"),
        ),
        check_vma=False,
    )
```

time: 280 us -> 202 us (0.72)
  waiting for transfers between devices: 161 us -> 84.6 us
  blocking collectives: 8.13 us -> 50.3 us
  Pallas kernels: 0 us -> 22.9 us
  starting transfers between devices: 52.6 us -> 33.3 us
  between operations: 15.2 us -> 1.31 us
  local copies, waits for them, and re-layouts: 22.6 us -> 8.79 us
  matrix products: 13.7 us -> 0 us
  other arithmetic: 6.24 us -> 0 us
    psum x1 -> x0, waiting for transfers between devices: 60.9 us -> none  [body(): lax.psum(up_part, 'dp').astype(jnp.float32)]
    all_to_all x0 -> x2, blocking collectives: none -> 50.3 us  [the longest x1 25.2 us: body(): part = lax.all_to_all(part, 'dp', split_axis=0, concat_axis=0, tiled=True)]
    pallas_call x0 -> x7, Pallas kernels: none -> 22.9 us  [call(): pl.pallas_call(kernel, out_shape=outs, in_specs=in_specs, out_specs=jax.t...]
    all_to_all x4 -> x2, starting transfers between devices: 52.4 us -> 33.3 us  [the longest x1 20.4 us: body(): lax.all_to_all(send.reshape(experts, CAP, 2 * quarter), 'expert', split_a...]
    all_to_all x4 -> x2, waiting for transfers between devices: 99.6 us -> 84.6 us  [the longest x1 50.4 us: body(): lax.all_to_all(send.reshape(experts, CAP, 2 * quarter), 'expert', split_a...]
    dot_general x10 -> x0, matrix products: 13.7 us -> none  [the longest x1 3.13 us: body(): jnp.dot(hidden, w_down, preferred_element_type=jnp.float32)]
    psum x1 -> x0, blocking collectives: 8.13 us -> none  [body(): grad_route_weights = lax.psum(gate_terms, 'dp')]
    unnamed x56 -> x3, local copies, waits for them, and re-layouts: 6.76 us -> 0.68 us
  transfers between devices with their start and end apart: 5 -> 2, of which waited for: 5 -> 2; matrix products, arithmetic and copies ran while one was open for 8% -> 0% of each run, Pallas kernels for 0% -> 4%
where the time goes in v1:
time: 202 us; the launch traced here: 201 us
  waiting for transfers between devices  84.6 us (42%)
  blocking collectives  50.3 us (25%)
  starting transfers between devices  33.3 us (16%)
  Pallas kernels  22.9 us (11%)
  local copies, waits for them, and re-layouts  8.79 us (4%)
    all_to_all x1, waiting for transfers between devices, body(): lax.all_to_all(send.reshape(experts, CAP, 2 * quarter), 'expert', split_a...  50.4 us
    all_to_all x1, waiting for transfers between devices, body(): lax.all_to_all(ret.reshape(experts, CAP, quarter + 128), 'expert', split_...  34.1 us
    all_to_all x1, blocking collectives, body(): part = lax.all_to_all(part, 'dp', split_axis=0, concat_axis=0, tiled=True)  25.2 us
    all_to_all x1, blocking collectives, body(): act = lax.all_to_all(act, 'dp', split_axis=0, concat_axis=0, tiled=True)  25.1 us
    pallas_call x7, Pallas kernels, call(): pl.pallas_call(kernel, out_shape=outs, in_specs=in_specs, out_specs=jax.t...  22.9 us
    all_to_all x1, starting transfers between devices, body(): lax.all_to_all(send.reshape(experts, CAP, 2 * quarter), 'expert', split_a...  20.4 us
    all_to_all x1, starting transfers between devices, body(): lax.all_to_all(ret.reshape(experts, CAP, quarter + 128), 'expert', split_...  12.9 us
  transfers between devices with their start and end apart: 2, of which 2 were waited for; matrix products, arithmetic and copies ran while one was open for 0% of the time, Pallas kernels for 4%

profile of v1, /device:TPU:1, one launch (start us, length us, event | category | flops | bytes accessed | tf_op | source)
XLA Modules:
  0.0 201.3 jit_solution(8038424061056497669)
XLA Ops:
  1.3 2.6 %shard_map.146 = (bf16[384,1024]{1,0:T(8,128)(2,1)}, bf16[384,128]{1,0:T(8,128)(2,1)}) custom-call(s32[1]{0:T(128)S(6)} %copy.18.live_ref, s32[2,128]{1,0:T(2,128)} %bitcast.3, f32[2,128]{1,0:T(2,128)} %bitcast.5, bf16[128,512]{1,0:T(8,128)(2,1)} %tokens_ref.1, bf16[128,512]{1,0:T(8,128)(2,1)} %grad_ref.1), custom_call_target="tpu_custom_call" | custom-call | flops 201326592 | bytes 786432 | tf_op jit(solution)/shard_map/pallas_call | solution.py:27
  3.9 0.0 copy-start
  3.9 3.3 %reshape.22 = bf16[128,3,1024]{2,1,0:T(4,128)(2,1)} reshape(bf16[384,1024]{1,0:T(8,128)(2,1)} %get-tuple-element.16) | data formatting | bytes 1572864 | tf_op jit(solution)/shard_map/reshape | solution.py:222
  7.1 20.4 %all-to-all-start = ((bf16[128,3,1024]{2,1,0:T(4,128)(2,1)}), bf16[128,3,1024]{2,1,0:T(4,128)(2,1)S(1)}, u32[]{:S(2)}, u32[]{:S(2)}) async-start(bf16[128,3,1024]{2,1,0:T(4,128)(2,1)} %reshape.22), calls=%async_computation | async-start | bytes 2097152 | tf_op jit(solution)/shard_map/all_to_all | solution.py:221
  27.5 0.0 copy-done
  27.5 0.7 copy.17.ds_ref
  28.2 3.3 %shard_map.147 = (bf16[512,768]{1,0:T(8,128)(2,1)}, bf16[512,768]{1,0:T(8,128)(2,1)}, bf16[768,512]{1,0:T(8,128)(2,1)}) custom-call(f32[4,6]{1,0:T(4,128)} %gs_ref.1, f32[4,6]{1,0:T(4,128)} %us_ref.1, f32[6,4]{1,0:T(8,128)} %copy.17.ds_ref, bf16[512,768]{1,0:T(8,128)(2,1)} %gc_ref.1, bf16[512,768]{1,0:T(8,128)(2,1)} %uc_ref.1, bf16[768,512]{1,0:T(8,128)(2,1)} %dc_ref.1), custom_call_target="tpu_custom_call" | custom-call | flops 1179648 | bytes 4718592 | tf_op jit(solution)/shard_map/pallas_call | solution.py:27
  31.5 50.4 %all-to-all-done = bf16[128,3,1024]{2,1,0:T(4,128)(2,1)S(1)} async-done(((bf16[128,3,1024]{2,1,0:T(4,128)(2,1)}), bf16[128,3,1024]{2,1,0:T(4,128)(2,1)S(1)}, u32[]{:S(2)}, u32[]{:S(2)}) %all-to-all-start) | async-done | bytes 786464 | tf_op jit(solution)/shard_map/all_to_all | solution.py:221
  81.9 1.4 reshape.23.rows_ref
  83.4 4.1 %shard_map.148 = bf16[4,288,768]{2,1,0:T(8,128)(2,1)} custom-call(bf16[384,1024]{1,0:T(8,128)(2,1)} %reshape.23.rows_ref, bf16[512,768]{1,0:T(8,128)(2,1)} %get-tuple-element.17.wg_ref, bf16[512,768]{1,0:T(8,128)(2,1)} %get-tuple-element.18.wu_ref, bf16[768,512]{1,0:T(8,128)(2,1)} %get-tuple-element.19.wd_ref), custom_call_target="tpu_custom_call" | custom-call | flops 905969664 | bytes 2359296 | tf_op jit(solution)/shard_map/pallas_call | solution.py:27
  87.5 25.2 %all_to_all.20.part_ref = bf16[4,288,768]{2,1,0:T(8,128)(2,1)} all-to-all(bf16[4,288,768]{2,1,0:T(8,128)(2,1)} %shard_map.148), channel_id=1, replica_groups=mesh['dp'=4,'expert'=128] {'dp'}, dimensions={0} | all-to-all | bytes 3538944 | tf_op jit(solution)/shard_map/all_to_all | solution.py:245
  112.7 3.3 %shard_map.149 = bf16[4,304,768]{2,1,0:T(8,128)(2,1)} custom-call(bf16[4,288,768]{2,1,0:T(8,128)(2,1)} %all_to_all.20.part_ref), custom_call_target="tpu_custom_call" | custom-call | flops 4423680 | bytes 4718592 | tf_op jit(solution)/shard_map/pallas_call | solution.py:27
  116.0 25.1 %all_to_all.21.act_ref = bf16[4,304,768]{2,1,0:T(8,128)(2,1)} all-to-all(bf16[4,304,768]{2,1,0:T(8,128)(2,1)} %shard_map.149), channel_id=1, replica_groups=mesh['dp'=4,'expert'=128] {'dp'}, dimensions={0} | all-to-all | bytes 3735552 | tf_op jit(solution)/shard_map/all_to_all | solution.py:254
  141.1 3.5 %shard_map.150 = bf16[384,640]{1,0:T(8,128)(2,1)} custom-call(bf16[4,304,768]{2,1,0:T(8,128)(2,1)} %all_to_all.21.act_ref, bf16[512,768]{1,0:T(8,128)(2,1)} %get-tuple-element.17.wg_ref, bf16[512,768]{1,0:T(8,128)(2,1)} %get-tuple-element.18.wu_ref), custom_call_target="tpu_custom_call" | custom-call | flops 603979776 | bytes 2359296 | tf_op jit(solution)/shard_map/pallas_call | solution.py:27
  144.7 2.2 %reshape.24 = bf16[128,3,640]{2,1,0:T(4,128)(2,1)} reshape(bf16[384,640]{1,0:T(8,128)(2,1)} %shard_map.150) | data formatting | bytes 983040 | tf_op jit(solution)/shard_map/reshape | solution.py:264
  146.9 12.9 %all-to-all-start.3 = ((bf16[128,3,640]{2,1,0:T(4,128)(2,1)}), bf16[128,3,640]{2,1,0:T(4,128)(2,1)S(1)}, u32[]{:S(2)}, u32[]{:S(2)}) async-start(bf16[128,3,640]{2,1,0:T(4,128)(2,1)} %reshape.24), calls=%async_computation.3 | async-start | bytes 1310720 | tf_op jit(solution)/shard_map/all_to_all | solution.py:263
  159.8 4.1 %shard_map.152 = (bf16[512,768]{1,0:T(8,128)(2,1)}, bf16[512,768]{1,0:T(8,128)(2,1)}, bf16[768,512]{1,0:T(8,128)(2,1)}) custom-call(bf16[384,1024]{1,0:T(8,128)(2,1)} %reshape.23.rows_ref, bf16[4,304,768]{2,1,0:T(8,128)(2,1)} %all_to_all.21.act_ref), custom_call_target="tpu_custom_call" | custom-call | flops 905969664 | bytes 4718592 | tf_op jit(solution)/shard_map/pallas_call | solution.py:27
  163.9 34.1 %all-to-all-done.3 = bf16[128,3,640]{2,1,0:T(4,128)(2,1)S(1)} async-done(((bf16[128,3,640]{2,1,0:T(4,128)(2,1)}), bf16[128,3,640]{2,1,0:T(4,128)(2,1)S(1)}, u32[]{:S(2)}, u32[]{:S(2)}) %all-to-all-start.3) | async-done | bytes 491552 | tf_op jit(solution)/shard_map/all_to_all | solution.py:263
  198.0 1.2 reshape.25.ret_ref
  199.2 2.0 %shard_map.151 = (bf16[128,512]{1,0:T(8,128)(2,1)}, f32[2,128]{1,0:T(2,128)}) custom-call(s32[2,128]{1,0:T(2,128)} %bitcast.4, f32[2,128]{1,0:T(2,128)} %bitcast.6, bf16[384,128]{1,0:T(8,128)(2,1)} %get-tuple-element.15.slots_ref, bf16[384,640]{1,0:T(8,128)(2,1)} %reshape.25.ret_ref), custom_call_target="tpu_custom_call" | custom-call | flops 50331648 | bytes 393216 | tf_op jit(solution)/shard_map/pallas_call | solution.py:27
Async XLA Ops:
  3.9 23.7 %copy-start = (f32[6,4]{0,1:T(4,128)S(1)}, f32[6,4]{0,1:T(4,128)}, u32[]{:S(2)}) copy-start(f32[6,4]{0,1:T(4,128)} %param.20) | copy-start | bytes 292
  7.1 74.8 %all-to-all-start = ((bf16[128,3,1024]{2,1,0:T(4,128)(2,1)}), bf16[128,3,1024]{2,1,0:T(4,128)(2,1)S(1)}, u32[]{:S(2)}, u32[]{:S(2)}) async-start(bf16[128,3,1024]{2,1,0:T(4,128)(2,1)} %reshape.22), calls=%async_computation | async-start | bytes 2097152 | tf_op jit(solution)/shard_map/all_to_all | solution.py:221
  146.9 51.1 %all-to-all-start.3 = ((bf16[128,3,640]{2,1,0:T(4,128)(2,1)}), bf16[128,3,640]{2,1,0:T(4,128)(2,1)S(1)}, u32[]{:S(2)}, u32[]{:S(2)}) async-start(bf16[128,3,640]{2,1,0:T(4,128)(2,1)} %reshape.24), calls=%async_computation.3 | async-start | bytes 1310720 | tf_op jit(solution)/shard_map/all_to_all | solution.py:263

commit v2 on v1

v2 whole, which is shorter than its diff:
```python
import jax
import jax.numpy as jnp
from jax import lax
from jax.experimental import pallas as pl
from jax.experimental.pallas import tpu as pltpu
from jax.sharding import PartitionSpec as P

BF = jnp.bfloat16
F32 = jnp.float32
CAP = 3
QPAD = 16
LANES = 128
GRANT = 24 << 20
LAST = (((1,), (1,)), ((), ()))
FIRST = (((0,), (0,)), ((), ()))
VMEM = pl.BlockSpec(memory_space=pltpu.VMEM)
SMEM = pl.BlockSpec(memory_space=pltpu.SMEM)


def split3(v):
    hi = v.astype(BF)
    rest = v - hi.astype(F32)
    mid = rest.astype(BF)
    lo = (rest - mid.astype(F32)).astype(BF)
    return hi, mid, lo


def call(kernel, outs, in_specs, args, flops=0, nbytes=0, scratch=()):
    return pl.pallas_call(
        kernel,
        out_shape=outs,
        in_specs=in_specs,
        out_specs=jax.tree.map(lambda _: VMEM, outs),
        scratch_shapes=scratch,
        compiler_params=pltpu.CompilerParams(vmem_limit_bytes=GRANT),
        cost_estimate=pl.CostEstimate(flops=flops, bytes_accessed=nbytes, transcendentals=0),
    )(*args)


def slot_kernel(live_ref, routes_ref, weights_ref, tokens_ref, grad_ref, send_ref, slots_ref, mix_ref):
    count, quarter = tokens_ref.shape
    experts = slots_ref.shape[0] // CAP
    wide = quarter // LANES
    chunks = 2 * CAP * wide
    expert = lax.broadcasted_iota(jnp.int32, (experts, count), 0)
    live = lax.broadcasted_iota(jnp.int32, (experts, count), 1) < live_ref[0]
    first = (routes_ref[0:1, :] == expert) & live
    second = (routes_ref[1:2, :] == expert) & live
    member = first | second
    before = (
        lax.broadcasted_iota(jnp.int32, (count, count), 0)
        < lax.broadcasted_iota(jnp.int32, (count, count), 1)
    ).astype(BF)
    ahead = jnp.dot(member.astype(BF), before, preferred_element_type=F32)
    weight = jnp.where(first, weights_ref[0:1, :], weights_ref[1:2, :])
    for p in range(CAP):
        chosen = member & (ahead == float(p))
        one_hot = chosen.astype(BF)
        slots_ref[p * experts : (p + 1) * experts, :] = one_hot
        picked = jnp.dot(one_hot, tokens_ref[...], preferred_element_type=F32)
        scaled = jnp.zeros((experts, quarter), F32)
        for piece in split3(jnp.where(chosen, weight, 0.0)):
            scaled = scaled + jnp.dot(piece, grad_ref[...], preferred_element_type=F32)
        for kind, value in enumerate((picked, scaled)):
            for h in range(wide):
                at = (kind * CAP + p) * wide + h
                mix_ref[pl.ds(at, experts, stride=chunks), :] = value[:, h * LANES : (h + 1) * LANES]
    send_ref[...] = mix_ref[...].astype(BF)


def dequant_kernel(gs_ref, us_ref, ds_ref, gc_ref, uc_ref, dc_ref, wg_ref, wu_ref, wd_ref):
    for scale_ref, code_ref, out_ref in (
        (gs_ref, gc_ref, wg_ref),
        (us_ref, uc_ref, wu_ref),
        (ds_ref, dc_ref, wd_ref),
    ):
        for i in range(scale_ref.shape[0]):
            for j in range(scale_ref.shape[1]):
                block = (slice(i * 128, i * 128 + 128), slice(j * 128, j * 128 + 128))
                out_ref[block] = (code_ref[block].astype(F32) * scale_ref[i, j]).astype(BF)


def partial_kernel(got_ref, wg_ref, wu_ref, wd_ref, part_ref, rows_ref, mix_ref):
    parts = part_ref.shape[0]
    quarter = wg_ref.shape[0]
    slots = rows_ref.shape[0]
    span = slots // parts
    groups = slots // CAP
    wide = quarter // LANES
    chunks = 2 * CAP * wide
    mix_ref[...] = got_ref[...].astype(F32)
    for kind in range(2):
        for p in range(CAP):
            for h in range(wide):
                at = (kind * CAP + p) * wide + h
                rows_ref[
                    p * groups : (p + 1) * groups, kind * quarter + h * LANES : kind * quarter + (h + 1) * LANES
                ] = mix_ref[pl.ds(at, groups, stride=chunks), :].astype(BF)
    token_rows = rows_ref[:, :quarter]
    for k, value in enumerate(
        (
            lambda: jnp.dot(token_rows, wg_ref[...], preferred_element_type=F32),
            lambda: jnp.dot(token_rows, wu_ref[...], preferred_element_type=F32),
            lambda: lax.dot_general(rows_ref[:, quarter:], wd_ref[...], LAST, preferred_element_type=F32),
        )
    ):
        result = value().astype(BF)
        for j in range(parts):
            part_ref[j, k * span : (k + 1) * span, :] = result[j * span : (j + 1) * span]


def act_kernel(part_ref, out_ref, hidden_ref):
    parts = part_ref.shape[0]
    span = part_ref.shape[1] // 3

    def total(k):
        lines = slice(k * span, (k + 1) * span)
        acc = part_ref[0, lines, :].astype(F32)
        for j in range(1, parts):
            acc = acc + part_ref[j, lines, :].astype(F32)
        return acc

    gate_pre, up_pre, grad_hidden = total(0), total(1), total(2)
    sig = jax.nn.sigmoid(gate_pre)
    activated = gate_pre * sig
    hidden = (activated * up_pre).astype(BF)
    gate_delta = (grad_hidden * up_pre * sig * (1.0 + gate_pre * (1.0 - sig))).astype(BF)
    up_delta = (grad_hidden * activated).astype(BF)
    prod = hidden.astype(F32) * grad_hidden
    prod = jnp.concatenate([prod, jnp.zeros((128 - span, prod.shape[1]), F32)], axis=0)
    ones = jnp.ones((QPAD, prod.shape[1]), BF)
    score = jnp.zeros((QPAD, 128), F32)
    for piece in split3(prod):
        score = score + lax.dot_general(ones, piece, LAST, preferred_element_type=F32)
    hi, mid, lo = split3(score)
    line = lax.broadcasted_iota(jnp.int32, (QPAD, 128), 0)
    scores = jnp.where(
        line == 0,
        hi.astype(F32),
        jnp.where(line == 1, mid.astype(F32), jnp.where(line == 2, lo.astype(F32), 0.0)),
    ).astype(BF)
    hidden_ref[...] = hidden
    for j in range(parts):
        out_ref[j, 0:span, :] = gate_delta
        out_ref[j, span : 2 * span, :] = up_delta
        out_ref[j, 2 * span : 2 * span + QPAD, 0:128] = scores


def back_kernel(act_ref, wg_ref, wu_ref, out_ref, mix_ref, score_ref):
    parts = act_ref.shape[0]
    span = (act_ref.shape[1] - QPAD) // 2
    quarter = wg_ref.shape[0]
    groups = parts * span // CAP
    wide = quarter // LANES
    chunks = out_ref.shape[0] // groups
    eye = (
        lax.broadcasted_iota(jnp.int32, (span, LANES), 0)
        == lax.broadcasted_iota(jnp.int32, (span, LANES), 1)
    ).astype(BF)
    for j in range(parts):
        scores = act_ref[j, 2 * span : 2 * span + QPAD, 0:LANES]
        scores = jnp.concatenate([scores, jnp.zeros((LANES - QPAD, LANES), BF)], axis=0)
        score_ref[j * span : (j + 1) * span, :] = lax.dot_general(
            eye, scores, LAST, preferred_element_type=F32
        )
    gate_delta = jnp.concatenate([act_ref[j, 0:span, :] for j in range(parts)], axis=0)
    up_delta = jnp.concatenate([act_ref[j, span : 2 * span, :] for j in range(parts)], axis=0)
    grad = lax.dot_general(gate_delta, wg_ref[...], LAST, preferred_element_type=F32)
    grad = grad + lax.dot_general(up_delta, wu_ref[...], LAST, preferred_element_type=F32)
    for p in range(CAP):
        lines = slice(p * groups, (p + 1) * groups)
        for h in range(wide):
            mix_ref[pl.ds(p * wide + h, groups, stride=chunks), :] = grad[lines, h * LANES : (h + 1) * LANES]
        mix_ref[pl.ds(CAP * wide + p, groups, stride=chunks), :] = score_ref[lines, :]
    for c in range(CAP * wide + CAP, chunks):
        mix_ref[pl.ds(c, groups, stride=chunks), :] = jnp.zeros((groups, LANES), F32)
    out_ref[...] = mix_ref[...].astype(BF)


def weight_grad_kernel(me_ref, rows_ref, act_ref, h0_ref, h1_ref, h2_ref, h3_ref, gg_ref, gu_ref, gd_ref):
    parts = act_ref.shape[0]
    span = (act_ref.shape[1] - QPAD) // 2
    quarter = gg_ref.shape[0]

    def gathered(k):
        return jnp.concatenate(
            [act_ref[j, k * span : (k + 1) * span, :] for j in range(parts)], axis=0
        )

    token_rows = rows_ref[:, :quarter]
    gg_ref[...] = lax.dot_general(
        token_rows, gathered(0), FIRST, preferred_element_type=F32
    ).astype(BF)
    gu_ref[...] = lax.dot_general(
        token_rows, gathered(1), FIRST, preferred_element_type=F32
    ).astype(BF)
    hidden, scaled = [], []
    for shift, ref in enumerate((h0_ref, h1_ref, h2_ref, h3_ref)):
        owner = lax.rem(me_ref[0] + parts - shift, parts)
        hidden.append(ref[...])
        scaled.append(rows_ref[pl.ds(pl.multiple_of(owner * span, span), span), quarter:])
    gd_ref[...] = lax.dot_general(
        jnp.concatenate(hidden, axis=0),
        jnp.concatenate(scaled, axis=0),
        FIRST,
        preferred_element_type=F32,
    ).astype(BF)


def home_kernel(routes_ref, weights_ref, slots_ref, ret_ref, grad_ref, score_ref, mix_ref):
    slots, count = slots_ref.shape
    experts = slots // CAP
    quarter = grad_ref.shape[1]
    wide = quarter // LANES
    chunks = ret_ref.shape[0] // experts
    mix_ref[...] = ret_ref[...].astype(F32)

    def chunk(c):
        return mix_ref[pl.ds(c, experts, stride=chunks), :]

    grad = jnp.zeros((count, quarter), F32)
    expert = lax.broadcasted_iota(jnp.int32, (experts, count), 0)
    scores = [jnp.zeros((1, count), F32)] * 2
    for p in range(CAP):
        one_hot = slots_ref[p * experts : (p + 1) * experts, :]
        block = jnp.concatenate([chunk(p * wide + h).astype(BF) for h in range(wide)], axis=1)
        grad = grad + lax.dot_general(one_hot, block, FIRST, preferred_element_type=F32)
        pieces = chunk(CAP * wide + p)
        picked = one_hot.astype(F32) * (pieces[:, 0:1] + pieces[:, 1:2] + pieces[:, 2:3])
        for k in range(2):
            mine = jnp.where(routes_ref[k : k + 1, :] == expert, picked, 0.0)
            scores[k] = scores[k] + jnp.sum(mine, axis=0, keepdims=True)
    grad_ref[...] = grad.astype(BF)
    for k in range(2):
        score_ref[k : k + 1, :] = scores[k] / weights_ref[k : k + 1, :]


def body(
    tokens,
    routes,
    route_weights,
    live_tokens,
    gate_codes,
    gate_scales,
    up_codes,
    up_scales,
    down_codes,
    down_scales,
    grad_out,
):
    count, quarter = tokens.shape
    hidden_size = gate_codes.shape[1]
    experts = lax.axis_size("expert")
    parts = lax.axis_size("dp")
    slots = experts * CAP
    span = slots // parts
    shape = jax.ShapeDtypeStruct
    routes_t = routes.T
    weights_t = route_weights.T

    wide = quarter // LANES
    out_chunks = 2 * CAP * wide
    back_chunks = -(-(CAP * wide + CAP) // 8) * 8
    me = lax.axis_index("dp")

    send, one_hot = call(
        slot_kernel,
        (shape((experts * out_chunks, LANES), BF), shape((slots, count), BF)),
        [SMEM, VMEM, VMEM, VMEM, VMEM],
        (live_tokens, routes_t, weights_t, tokens, grad_out),
        flops=2 * slots * count * quarter * 4,
        nbytes=2 * slots * 2 * quarter,
        scratch=[pltpu.VMEM((experts * out_chunks, LANES), F32)],
    )
    got = lax.all_to_all(
        send.reshape(experts, out_chunks, LANES), "expert", split_axis=0, concat_axis=0, tiled=True
    )
    w_gate, w_up, w_down = call(
        dequant_kernel,
        (
            shape(gate_codes.shape, BF),
            shape(up_codes.shape, BF),
            shape(down_codes.shape, BF),
        ),
        [SMEM] * 3 + [VMEM] * 3,
        (gate_scales, up_scales, down_scales, gate_codes, up_codes, down_codes),
        flops=3 * quarter * hidden_size,
        nbytes=12 * quarter * hidden_size,
    )
    part, rows = call(
        partial_kernel,
        (shape((parts, 3 * span, hidden_size), BF), shape((slots, 2 * quarter), BF)),
        [VMEM] * 4,
        (got.reshape(experts * out_chunks, LANES), w_gate, w_up, w_down),
        flops=6 * slots * quarter * hidden_size,
        nbytes=8 * slots * hidden_size,
        scratch=[pltpu.VMEM((experts * out_chunks, LANES), F32)],
    )
    part = lax.all_to_all(part, "dp", split_axis=0, concat_axis=0, tiled=True)
    act, hidden = call(
        act_kernel,
        (shape((parts, 2 * span + QPAD, hidden_size), BF), shape((span, hidden_size), BF)),
        [VMEM],
        (part,),
        flops=60 * span * hidden_size,
        nbytes=16 * slots * hidden_size,
    )
    act = lax.all_to_all(act, "dp", split_axis=0, concat_axis=0, tiled=True)
    ret = call(
        back_kernel,
        shape((experts * back_chunks, LANES), BF),
        [VMEM] * 3,
        (act, w_gate, w_up),
        flops=4 * slots * quarter * hidden_size,
        nbytes=8 * slots * hidden_size,
        scratch=[
            pltpu.VMEM((experts * back_chunks, LANES), F32),
            pltpu.VMEM((slots, LANES), F32),
        ],
    )
    ret, hidden = lax.optimization_barrier((ret, hidden))
    ret = lax.all_to_all(
        ret.reshape(experts, back_chunks, LANES), "expert", split_axis=0, concat_axis=0, tiled=True
    )
    others = [
        lax.ppermute(hidden, "dp", [(i, (i + shift) % parts) for i in range(parts)])
        for shift in range(1, parts)
    ]
    grad_gate, grad_up, grad_down = call(
        weight_grad_kernel,
        (
            shape((quarter, hidden_size), BF),
            shape((quarter, hidden_size), BF),
            shape((hidden_size, quarter), BF),
        ),
        [SMEM] + [VMEM] * 6,
        (me.reshape(1), rows, act, hidden, *others),
        flops=6 * slots * quarter * hidden_size,
        nbytes=16 * slots * hidden_size,
    )
    grad_tokens, grad_weights_t = call(
        home_kernel,
        (shape((count, quarter), BF), shape((2, count), F32)),
        [VMEM] * 4,
        (routes_t, weights_t, one_hot, ret.reshape(experts * back_chunks, LANES)),
        flops=2 * slots * count * quarter,
        nbytes=2 * slots * quarter,
        scratch=[pltpu.VMEM((experts * back_chunks, LANES), F32)],
    )
    return (grad_tokens, grad_weights_t.T, grad_gate, grad_up, grad_down)


def solution(mesh):
    placed = (
        P("expert", "dp"),
        P("expert", None),
        P("expert", None),
        P("expert"),
        P("dp", "expert"),
        P("dp", "expert"),
        P("dp", "expert"),
        P("dp", "expert"),
        P("expert", "dp"),
        P("expert", "dp"),
        P("expert", "dp"),
    )
    return jax.shard_map(
        body,
        mesh=mesh,
        in_specs=placed,
        out_specs=(
            P("expert", "dp"),
            P("expert", None),
            P("dp", "expert"),
            P("dp", "expert"),
            P("expert", "dp"),
        ),
        check_vma=False,
    )
```

time: 202 us -> 166 us (0.82)
  waiting for transfers between devices: 84.6 us -> 60.6 us
  Pallas kernels: 22.9 us -> 10 us
  blocking collectives: 50.3 us -> 41.9 us
  starting transfers between devices: 33.3 us -> 40.9 us
    all_to_all x2, waiting for transfers between devices: 84.6 us -> 55.4 us  [the longest x1 39.3 us: body(): lax.all_to_all(send.reshape(experts, out_chunks, LANES), 'expert', split_...]
    pallas_call x7, Pallas kernels: 22.9 us -> 10 us  [call(): pl.pallas_call(kernel, out_shape=outs, in_specs=in_specs, out_specs=jax.t...]
    unnamed x3 -> x39, local copies, waits for them, and re-layouts: 0.68 us -> 10.4 us
    ppermute x0 -> x3, starting transfers between devices: none -> 8.43 us  [body(): lax.ppermute(hidden, 'dp', [(i, (i + shift) % parts) for i in range(parts)])]
    reshape x4 -> x0, local copies, waits for them, and re-layouts: 8.11 us -> none  [the longest x1 3.29 us: body(): send.reshape(experts, CAP, 2 * quarter)]
    all_to_all x1, blocking collectives: 25.1 us -> 17.1 us  [body(): act = lax.all_to_all(act, 'dp', split_axis=0, concat_axis=0, tiled=True)]
    ppermute x0 -> x3, waiting for transfers between devices: none -> 5.2 us  [body(): lax.ppermute(hidden, 'dp', [(i, (i + shift) % parts) for i in range(parts)])]
  transfers between devices with their start and end apart: 2 -> 5, of which waited for: 2 -> 4; matrix products, arithmetic and copies ran while one was open for 0% -> 0% of each run, Pallas kernels for 4% -> 2%
where the time goes in v2:
time: 166 us; the launch traced here: 165 us
  waiting for transfers between devices  60.6 us (37%)
  blocking collectives  41.9 us (25%)
  starting transfers between devices  40.9 us (25%)
  local copies, waits for them, and re-layouts  10.4 us (6%)
  Pallas kernels  10 us (6%)
    all_to_all x1, waiting for transfers between devices, body(): lax.all_to_all(send.reshape(experts, out_chunks, LANES), 'expert', split_...  39.3 us
    all_to_all x1, blocking collectives, body(): part = lax.all_to_all(part, 'dp', split_axis=0, concat_axis=0, tiled=True)  24.8 us
    all_to_all x1, starting transfers between devices, body(): lax.all_to_all(send.reshape(experts, out_chunks, LANES), 'expert', split_...  20.4 us
    all_to_all x1, blocking collectives, body(): act = lax.all_to_all(act, 'dp', split_axis=0, concat_axis=0, tiled=True)  17.1 us
    all_to_all x1, waiting for transfers between devices, body(): lax.all_to_all(ret.reshape(experts, back_chunks, LANES), 'expert', split_...  16 us
    all_to_all x1, starting transfers between devices, body(): lax.all_to_all(ret.reshape(experts, back_chunks, LANES), 'expert', split_...  12.1 us
    unnamed x39, local copies, waits for them, and re-layouts  10.4 us
    pallas_call x7, Pallas kernels, call(): pl.pallas_call(kernel, out_shape=outs, in_specs=in_specs, out_specs=jax.t...  10 us
  transfers between devices with their start and end apart: 5, of which 4 were waited for; matrix products, arithmetic and copies ran while one was open for 0% of the time, Pallas kernels for 2%

profile of v2, /device:TPU:1, one launch (start us, length us, event | category | flops | bytes accessed | tf_op | source)
XLA Modules:
  0.0 165.5 jit_solution(7847013861288765713)
XLA Ops:
  0.6 0.0 copy-start.6
  0.6 0.0 copy-start.7
  0.7 0.0 copy-start
  0.7 0.0 copy-start.1
  1.4 0.0 copy-start.8
  1.5 0.7 copy-done.8
  2.1 0.7 copy-done.10
  2.8 0.9 copy-done.14
  3.7 0.9 copy-done.15
  4.6 1.7 shard_map.146
  6.3 20.4 %all-to-all-start = ((bf16[128,24,128]{2,1,0:T(8,128)(2,1)}), bf16[128,24,128]{2,1,0:T(8,128)(2,1)S(1)}, u32[]{:S(2)}, u32[]{:S(2)}) async-start(bf16[128,24,128]{2,1,0:T(8,128)(2,1)} %bitcast.2), calls=%async_computation | async-start | bytes 1572864 | tf_op jit(solution)/shard_map/all_to_all | solution.py:275
  26.7 0.0 copy-done.18
  26.7 0.1 copy.16.ds_ref
  26.8 0.0 copy-done.6
  26.8 0.0 copy-done.7
  26.8 0.0 copy-done
  26.8 0.0 copy-done.1
  26.8 0.0 copy-start.2
  26.8 1.1 copy-done.2
  27.9 1.1 shard_map.147
  29.0 0.0 copy-start.3
  29.1 0.9 copy-done.3
  29.9 0.9 copy-done.12
  30.8 39.3 %all-to-all-done = bf16[128,24,128]{2,1,0:T(8,128)(2,1)S(1)} async-done(((bf16[128,24,128]{2,1,0:T(8,128)(2,1)}), bf16[128,24,128]{2,1,0:T(8,128)(2,1)S(1)}, u32[]{:S(2)}, u32[]{:S(2)}) %all-to-all-start) | async-done | bytes 786464 | tf_op jit(solution)/shard_map/all_to_all | solution.py:275
  70.1 1.1 copy-done.4
  71.3 1.1 copy-done.13
  72.4 1.3 shard_map.148
  73.7 0.0 copy-start.16
  73.7 0.9 copy-done.16
  74.6 24.8 %all_to_all.20.part_ref = bf16[4,288,768]{2,1,0:T(8,128)(2,1)S(1)} all-to-all(bf16[4,288,768]{2,1,0:T(8,128)(2,1)S(1)} %get-tuple-element.26), channel_id=1, replica_groups=mesh['dp'=4,'expert'=128] {'dp'}, dimensions={0} | all-to-all | bytes 3538944 | tf_op jit(solution)/shard_map/all_to_all | solution.py:299
  99.4 0.6 shard_map.149
  100.0 17.1 %all_to_all.21.act_ref = bf16[4,208,768]{2,1,0:T(8,128)(2,1)S(1)} all-to-all(bf16[4,208,768]{2,1,0:T(8,128)(2,1)S(1)} %get-tuple-element.27), channel_id=1, replica_groups=mesh['dp'=4,'expert'=128] {'dp'}, dimensions={0} | all-to-all | bytes 2555904 | tf_op jit(solution)/shard_map/all_to_all | solution.py:308
  117.1 0.0 copy-done.5
  117.1 1.9 %shard_map.150 = bf16[2048,128]{1,0:T(8,128)(2,1)} custom-call(bf16[4,208,768]{2,1,0:T(8,128)(2,1)S(1)} %all_to_all.21.act_ref, bf16[512,768]{1,0:T(8,128)(2,1)S(1)} %get-tuple-element.23.wg_ref, bf16[512,768]{1,0:T(8,128)(2,1)S(1)} %copy-done.5), custom_call_target="tpu_custom_call" | custom-call | flops 603979776 | bytes 2359296 | tf_op jit(solution)/shard_map/pallas_call | solution.py:29
  119.0 12.1 %all-to-all-start.3 = ((bf16[128,16,128]{2,1,0:T(8,128)(2,1)}), bf16[128,16,128]{2,1,0:T(8,128)(2,1)S(1)}, u32[]{:S(2)}, u32[]{:S(2)}) async-start(bf16[128,16,128]{2,1,0:T(8,128)(2,1)} %bitcast.4), calls=%async_computation.3 | async-start | bytes 1048576 | tf_op jit(solution)/shard_map/all_to_all | solution.py:322
  131.1 0.0 copy-start.9
  131.1 0.0 copy-start.11
  131.1 2.2 %collective-permute-start = (bf16[96,768]{1,0:T(8,128)(2,1)S(1)}, bf16[96,768]{1,0:T(8,128)(2,1)S(1)}, u32[]{:S(2)}, u32[]{:S(2)}) collective-permute-start(bf16[96,768]{1,0:T(8,128)(2,1)S(1)} %get-tuple-element.33.h0_ref), channel_id=1, source_target_pairs={{0,128},{128,256},{256,384},{384,0},{1,129},{129,257},{257,385},{3... | collective-permute-start | bytes 442376 | tf_op jit(solution)/shard_map/ppermute | solution.py:326
  133.3 3.7 %collective-permute-start.1 = (bf16[96,768]{1,0:T(8,128)(2,1)S(1)}, bf16[96,768]{1,0:T(8,128)(2,1)S(1)}, u32[]{:S(2)}, u32[]{:S(2)}) collective-permute-start(bf16[96,768]{1,0:T(8,128)(2,1)S(1)} %get-tuple-element.33.h0_ref), channel_id=1, source_target_pairs={{0,256},{128,384},{256,0},{384,128},{1,257},{129,385},{257,1},{385... | collective-permute-start | bytes 442376 | tf_op jit(solution)/shard_map/ppermute | solution.py:326
  137.0 2.5 %collective-permute-start.2 = (bf16[96,768]{1,0:T(8,128)(2,1)S(1)}, bf16[96,768]{1,0:T(8,128)(2,1)S(1)}, u32[]{:S(2)}, u32[]{:S(2)}) collective-permute-start(bf16[96,768]{1,0:T(8,128)(2,1)S(1)} %get-tuple-element.33.h0_ref), channel_id=1, source_target_pairs={{0,384},{128,0},{256,128},{384,256},{1,385},{129,1},{257,129},{385... | collective-permute-start | bytes 442376 | tf_op jit(solution)/shard_map/ppermute | solution.py:326
  139.6 0.0 collective-permute-done.h1_ref
  139.6 1.6 collective-permute-done.1.h2_ref
  141.2 3.6 %collective-permute-done.2.h3_ref = bf16[96,768]{1,0:T(8,128)(2,1)S(1)} collective-permute-done((bf16[96,768]{1,0:T(8,128)(2,1)S(1)}, bf16[96,768]{1,0:T(8,128)(2,1)S(1)}, u32[]{:S(2)}, u32[]{:S(2)}) %collective-permute-start.2) | collective-permute-done | bytes 147488 | tf_op jit(solution)/shard_map/ppermute | solution.py:326
  144.8 1.1 copy-done.17
  145.9 2.3 %shard_map.152 = (bf16[512,768]{1,0:T(8,128)(2,1)}, bf16[512,768]{1,0:T(8,128)(2,1)}, bf16[768,512]{1,0:T(8,128)(2,1)}) custom-call(s32[1]{0:T(128)} %bitcast.7.me_ref, bf16[384,1024]{1,0:T(8,128)(2,1)S(1)} %copy-done.17, bf16[4,208,768]{2,1,0:T(8,128)(2,1)S(1)} %all_to_all.21.act_ref, bf16[96,768]{1,0:T(8,128)(2,1)S(1)} %get-tuple-element.33.h0_ref, ...), custom_call_target="tpu_custom_call" | custom-call | flops 905969664 | bytes 4718592 | tf_op jit(solution)/shard_map/pallas_call | solution.py:29
  148.3 16.0 %all-to-all-done.3 = bf16[128,16,128]{2,1,0:T(8,128)(2,1)S(1)} async-done(((bf16[128,16,128]{2,1,0:T(8,128)(2,1)}), bf16[128,16,128]{2,1,0:T(8,128)(2,1)S(1)}, u32[]{:S(2)}, u32[]{:S(2)}) %all-to-all-start.3) | async-done | bytes 524320 | tf_op jit(solution)/shard_map/all_to_all | solution.py:322
  164.3 0.0 copy-done.9
  164.3 1.2 shard_map.151
  (10 shorter events, 0.0 us)
Async XLA Ops:
  0.6 26.1 %copy-start.6 = (f32[4,6]{1,0:T(4,128)S(1)}, f32[4,6]{1,0:T(4,128)}, u32[]{:S(2)}) copy-start(f32[4,6]{1,0:T(4,128)} %gs_ref.1) | copy-start | bytes 292
  0.6 26.1 %copy-start.7 = (f32[4,6]{1,0:T(4,128)S(1)}, f32[4,6]{1,0:T(4,128)}, u32[]{:S(2)}) copy-start(f32[4,6]{1,0:T(4,128)} %us_ref.1) | copy-start | bytes 292
  0.7 26.1 %copy-start = (bf16[512,768]{1,0:T(8,128)(2,1)S(1)}, bf16[512,768]{1,0:T(8,128)(2,1)}, u32[]{:S(2)}) copy-start(bf16[512,768]{1,0:T(8,128)(2,1)} %gc_ref.1) | copy-start | bytes 2359300
  0.7 26.1 %copy-start.1 = (bf16[512,768]{1,0:T(8,128)(2,1)S(1)}, bf16[512,768]{1,0:T(8,128)(2,1)}, u32[]{:S(2)}) copy-start(bf16[512,768]{1,0:T(8,128)(2,1)} %uc_ref.1) | copy-start | bytes 2359300
  1.4 0.7 copy-start.8
  2.1 0.7 copy-start.10
  2.8 0.9 copy-start.14
  3.7 0.9 copy-start.15
  4.6 22.1 %copy-start.18 = (f32[6,4]{0,1:T(4,128)S(1)}, f32[6,4]{0,1:T(4,128)}, u32[]{:S(2)}) copy-start(f32[6,4]{0,1:T(4,128)} %param.20) | copy-start | bytes 292
  6.3 63.9 %all-to-all-start = ((bf16[128,24,128]{2,1,0:T(8,128)(2,1)}), bf16[128,24,128]{2,1,0:T(8,128)(2,1)S(1)}, u32[]{:S(2)}, u32[]{:S(2)}) async-start(bf16[128,24,128]{2,1,0:T(8,128)(2,1)} %bitcast.2), calls=%async_computation | async-start | bytes 1572864 | tf_op jit(solution)/shard_map/all_to_all | solution.py:275
  26.8 1.1 copy-start.2
  29.0 0.9 copy-start.3
  29.9 0.9 copy-start.12
  70.1 1.1 copy-start.4
  71.3 1.1 copy-start.13
  73.7 0.9 copy-start.16
  99.4 17.7 %copy-start.5 = (bf16[512,768]{1,0:T(8,128)(2,1)S(1)}, bf16[512,768]{1,0:T(8,128)(2,1)}, u32[]{:S(2)}) copy-start(bf16[512,768]{1,0:T(8,128)(2,1)} %copy-done.3) | copy-start | bytes 2359300
  119.0 45.3 %all-to-all-start.3 = ((bf16[128,16,128]{2,1,0:T(8,128)(2,1)}), bf16[128,16,128]{2,1,0:T(8,128)(2,1)S(1)}, u32[]{:S(2)}, u32[]{:S(2)}) async-start(bf16[128,16,128]{2,1,0:T(8,128)(2,1)} %bitcast.4), calls=%async_computation.3 | async-start | bytes 1048576 | tf_op jit(solution)/shard_map/all_to_all | solution.py:322
  131.1 33.2 %copy-start.9 = (s32[128,2]{0,1:T(2,128)S(1)}, s32[128,2]{0,1:T(2,128)}, u32[]{:S(2)}) copy-start(s32[128,2]{0,1:T(2,128)} %param.12) | copy-start | bytes 3076
  131.1 33.2 %copy-start.11 = (f32[128,2]{0,1:T(2,128)S(1)}, f32[128,2]{0,1:T(2,128)}, u32[]{:S(2)}) copy-start(f32[128,2]{0,1:T(2,128)} %param.13) | copy-start | bytes 3076
  131.1 8.5 %collective-permute-start = (bf16[96,768]{1,0:T(8,128)(2,1)S(1)}, bf16[96,768]{1,0:T(8,128)(2,1)S(1)}, u32[]{:S(2)}, u32[]{:S(2)}) collective-permute-start(bf16[96,768]{1,0:T(8,128)(2,1)S(1)} %get-tuple-element.33.h0_ref), channel_id=1, source_target_pairs={{0,128},{128,256},{256,384},{384,0},{1,129},{129,257},{257,385},{3... | collective-permute-start | bytes 442376 | tf_op jit(solution)/shard_map/ppermute | solution.py:326
  133.3 7.8 %collective-permute-start.1 = (bf16[96,768]{1,0:T(8,128)(2,1)S(1)}, bf16[96,768]{1,0:T(8,128)(2,1)S(1)}, u32[]{:S(2)}, u32[]{:S(2)}) collective-permute-start(bf16[96,768]{1,0:T(8,128)(2,1)S(1)} %get-tuple-element.33.h0_ref), channel_id=1, source_target_pairs={{0,256},{128,384},{256,0},{384,128},{1,257},{129,385},{257,1},{385... | collective-permute-start | bytes 442376 | tf_op jit(solution)/shard_map/ppermute | solution.py:326
  137.0 7.8 %collective-permute-start.2 = (bf16[96,768]{1,0:T(8,128)(2,1)S(1)}, bf16[96,768]{1,0:T(8,128)(2,1)S(1)}, u32[]{:S(2)}, u32[]{:S(2)}) collective-permute-start(bf16[96,768]{1,0:T(8,128)(2,1)S(1)} %get-tuple-element.33.h0_ref), channel_id=1, source_target_pairs={{0,384},{128,0},{256,128},{384,256},{1,385},{129,1},{257,129},{385... | collective-permute-start | bytes 442376 | tf_op jit(solution)/shard_map/ppermute | solution.py:326
  144.8 1.1 copy-start.17

commit v3 on v2

v3 whole, which is shorter than its diff:
```python
import jax
import jax.numpy as jnp
from jax import lax
from jax.experimental import pallas as pl
from jax.experimental.pallas import tpu as pltpu
from jax.sharding import PartitionSpec as P


BF = jnp.bfloat16
F32 = jnp.float32
CAP = 3
LANES = 128
GRANT = 24 << 20
WIDE = 60 << 20
LAST = (((1,), (1,)), ((), ()))
FIRST = (((0,), (0,)), ((), ()))
VMEM = pl.BlockSpec(memory_space=pltpu.VMEM)
SMEM = pl.BlockSpec(memory_space=pltpu.SMEM)


def split3(v):
    hi = v.astype(BF)
    rest = v - hi.astype(F32)
    mid = rest.astype(BF)
    lo = (rest - mid.astype(F32)).astype(BF)
    return hi, mid, lo


def call(kernel, outs, in_specs, args, flops=0, nbytes=0, scratch=(), grant=GRANT):
    return pl.pallas_call(
        kernel,
        out_shape=outs,
        in_specs=in_specs,
        out_specs=jax.tree.map(lambda _: VMEM, outs),
        scratch_shapes=scratch,
        compiler_params=pltpu.CompilerParams(vmem_limit_bytes=grant),
        cost_estimate=pl.CostEstimate(flops=flops, bytes_accessed=nbytes, transcendentals=0),
    )(*args)


def slot_kernel(live_ref, routes_ref, weights_ref, tokens_ref, grad_ref, send_ref, slots_ref, mix_ref):
    count, quarter = tokens_ref.shape
    experts = slots_ref.shape[0] // CAP
    wide = quarter // LANES
    chunks = 2 * CAP * wide
    expert = lax.broadcasted_iota(jnp.int32, (experts, count), 0)
    live = lax.broadcasted_iota(jnp.int32, (experts, count), 1) < live_ref[0]
    first = (routes_ref[0:1, :] == expert) & live
    second = (routes_ref[1:2, :] == expert) & live
    member = first | second
    before = (
        lax.broadcasted_iota(jnp.int32, (count, count), 0)
        < lax.broadcasted_iota(jnp.int32, (count, count), 1)
    ).astype(BF)
    ahead = jnp.dot(member.astype(BF), before, preferred_element_type=F32)
    weight = jnp.where(first, weights_ref[0:1, :], weights_ref[1:2, :])
    for p in range(CAP):
        chosen = member & (ahead == float(p))
        one_hot = chosen.astype(BF)
        slots_ref[p * experts : (p + 1) * experts, :] = one_hot
        picked = jnp.dot(one_hot, tokens_ref[...], preferred_element_type=F32)
        scaled = jnp.zeros((experts, quarter), F32)
        for piece in split3(jnp.where(chosen, weight, 0.0)):
            scaled = scaled + jnp.dot(piece, grad_ref[...], preferred_element_type=F32)
        for kind, value in enumerate((picked, scaled)):
            for h in range(wide):
                at = (kind * CAP + p) * wide + h
                mix_ref[pl.ds(at, experts, stride=chunks), :] = value[:, h * LANES : (h + 1) * LANES]
    send_ref[...] = mix_ref[...].astype(BF)


def dequant(scale_ref, code_ref, out_ref, base):
    for i in range(scale_ref.shape[0]):
        for j in range(scale_ref.shape[1]):
            lines = slice(i * LANES, (i + 1) * LANES)
            lanes = slice(j * LANES, (j + 1) * LANES)
            out_ref[base + i * LANES : base + (i + 1) * LANES, lanes] = (
                code_ref[lines, lanes].astype(F32) * scale_ref[i, j]
            ).astype(BF)


def dequant_pair_kernel(gs_ref, us_ref, gc_ref, uc_ref, out_ref):
    dequant(gs_ref, gc_ref, out_ref, 0)
    dequant(us_ref, uc_ref, out_ref, gc_ref.shape[0])


def dequant_one_kernel(ds_ref, dc_ref, out_ref):
    dequant(ds_ref, dc_ref, out_ref, 0)


def row_kernel(got_ref, wd_ref, out_ref, rows_ref, mix_ref):
    parts, span, _ = out_ref.shape
    quarter = rows_ref.shape[1] // 2
    groups = rows_ref.shape[0] // CAP
    wide = quarter // LANES
    chunks = 2 * CAP * wide
    mix_ref[...] = got_ref[...].astype(F32)
    for kind in range(2):
        for p in range(CAP):
            for h in range(wide):
                at = (kind * CAP + p) * wide + h
                lane = kind * quarter + h * LANES
                rows_ref[p * groups : (p + 1) * groups, lane : lane + LANES] = mix_ref[
                    pl.ds(at, groups, stride=chunks), :
                ].astype(BF)
    back = lax.dot_general(
        rows_ref[:, quarter:], wd_ref[...], LAST, preferred_element_type=F32
    ).astype(BF)
    for j in range(parts):
        lines = slice(j * span, (j + 1) * span)
        out_ref[j, :, :quarter] = rows_ref[lines, :quarter]
        out_ref[j, :, quarter:] = back[lines]


def act_kernel(me_ref, part_ref, own_ref, next_ref, far_ref, prev_ref, out_ref, act_ref):
    parts, span, _ = part_ref.shape
    quarter = own_ref.shape[0] // 2
    owners = [lax.rem(me_ref[0] + shift, parts) for shift in range(parts)]

    blocks = (own_ref, next_ref, far_ref, prev_ref)

    def gate_of(shift):
        return blocks[shift][:quarter, :]

    def up_of(shift):
        return blocks[shift][quarter:, :]

    gate_pre = up_pre = 0.0
    for shift in range(parts):
        token_rows = part_ref[owners[shift], :, :quarter]
        gate = jnp.dot(token_rows, gate_of(shift), preferred_element_type=F32)
        gate_pre = gate_pre + gate.astype(BF).astype(F32)
        up = jnp.dot(token_rows, up_of(shift), preferred_element_type=F32)
        up_pre = up_pre + up.astype(BF).astype(F32)
    grad_hidden = part_ref[0, :, quarter:].astype(F32)
    for j in range(1, parts):
        grad_hidden = grad_hidden + part_ref[j, :, quarter:].astype(F32)
    sig = jax.nn.sigmoid(gate_pre)
    activated = gate_pre * sig
    hidden = (activated * up_pre).astype(BF)
    gate_delta = (grad_hidden * up_pre * sig * (1.0 + gate_pre * (1.0 - sig))).astype(BF)
    up_delta = (grad_hidden * activated).astype(BF)
    act_ref[0:span, :] = gate_delta
    act_ref[span : 2 * span, :] = up_delta
    act_ref[2 * span : 3 * span, :] = hidden
    score = jnp.sum(hidden.astype(F32) * grad_hidden, axis=1, keepdims=True)
    lane = lax.broadcasted_iota(jnp.int32, (span, LANES), 1)
    hi, mid, lo = (v.astype(F32) for v in split3(score))
    scores = jnp.where(
        lane == 0, hi, jnp.where(lane == 1, mid, jnp.where(lane == 2, lo, 0.0))
    ).astype(BF)
    for shift in range(parts):
        grad = lax.dot_general(gate_delta, gate_of(shift), LAST, preferred_element_type=F32)
        grad = grad + lax.dot_general(up_delta, up_of(shift), LAST, preferred_element_type=F32)
        out_ref[owners[shift], :, :quarter] = grad.astype(BF)
        out_ref[owners[shift], :, quarter:] = scores


def pack_kernel(grad_ref, out_ref, mix_ref):
    groups = grad_ref.shape[0] // CAP
    wide = grad_ref.shape[1] // LANES - 1
    chunks = out_ref.shape[0] // groups
    for p in range(CAP):
        for h in range(wide + 1):
            at = p * wide + h if h < wide else CAP * wide + p
            mix_ref[pl.ds(at, groups, stride=chunks), :] = grad_ref[
                p * groups : (p + 1) * groups, h * LANES : (h + 1) * LANES
            ].astype(F32)
    for c in range(CAP * wide + CAP, chunks):
        mix_ref[pl.ds(c, groups, stride=chunks), :] = jnp.zeros((groups, LANES), F32)
    out_ref[...] = mix_ref[...].astype(BF)


def weight_grad_kernel(me_ref, rows_ref, a0_ref, a1_ref, a2_ref, a3_ref, gg_ref, gu_ref, gd_ref):
    parts = 4
    span = a0_ref.shape[0] // 3
    quarter = gg_ref.shape[0]
    rows, acts = [], []
    for shift, ref in enumerate((a0_ref, a1_ref, a2_ref, a3_ref)):
        owner = lax.rem(me_ref[0] + parts - shift, parts)
        rows.append(rows_ref[pl.ds(pl.multiple_of(owner * span, span), span), :])
        acts.append(ref)
    rows = jnp.concatenate(rows, axis=0)

    def gathered(k):
        return jnp.concatenate([ref[k * span : (k + 1) * span, :] for ref in acts], axis=0)

    token_rows = rows[:, :quarter]
    gg_ref[...] = lax.dot_general(
        token_rows, gathered(0), FIRST, preferred_element_type=F32
    ).astype(BF)
    gu_ref[...] = lax.dot_general(
        token_rows, gathered(1), FIRST, preferred_element_type=F32
    ).astype(BF)
    gd_ref[...] = lax.dot_general(
        gathered(2), rows[:, quarter:], FIRST, preferred_element_type=F32
    ).astype(BF)


def home_kernel(routes_ref, weights_ref, slots_ref, ret_ref, grad_ref, score_ref, mix_ref):
    slots, count = slots_ref.shape
    experts = slots // CAP
    quarter = grad_ref.shape[1]
    wide = quarter // LANES
    chunks = ret_ref.shape[0] // experts
    mix_ref[...] = ret_ref[...].astype(F32)

    def chunk(c):
        return mix_ref[pl.ds(c, experts, stride=chunks), :]

    grad = jnp.zeros((count, quarter), F32)
    expert = lax.broadcasted_iota(jnp.int32, (experts, count), 0)
    scores = [jnp.zeros((1, count), F32)] * 2
    for p in range(CAP):
        one_hot = slots_ref[p * experts : (p + 1) * experts, :]
        block = jnp.concatenate([chunk(p * wide + h).astype(BF) for h in range(wide)], axis=1)
        grad = grad + lax.dot_general(one_hot, block, FIRST, preferred_element_type=F32)
        pieces = chunk(CAP * wide + p)
        picked = one_hot.astype(F32) * (pieces[:, 0:1] + pieces[:, 1:2] + pieces[:, 2:3])
        for k in range(2):
            mine = jnp.where(routes_ref[k : k + 1, :] == expert, picked, 0.0)
            scores[k] = scores[k] + jnp.sum(mine, axis=0, keepdims=True)
    grad_ref[...] = grad.astype(BF)
    for k in range(2):
        score_ref[k : k + 1, :] = scores[k] / weights_ref[k : k + 1, :]


def layer(
    tokens,
    routes,
    route_weights,
    live_tokens,
    gate_codes,
    gate_scales,
    up_codes,
    up_scales,
    down_codes,
    down_scales,
    grad_out,
):
    count, quarter = tokens.shape
    hidden_size = gate_codes.shape[1]
    experts = lax.axis_size("expert")
    parts = lax.axis_size("dp")
    slots = experts * CAP
    span = slots // parts
    shape = jax.ShapeDtypeStruct
    routes_t = routes.T
    weights_t = route_weights.T

    wide = quarter // LANES
    out_chunks = 2 * CAP * wide
    back_chunks = -(-(CAP * wide + CAP) // 8) * 8
    me = lax.axis_index("dp")

    def turn(value, shift):
        return lax.ppermute(value, "dp", [(i, (i + shift) % parts) for i in range(parts)])

    w_own = call(
        dequant_pair_kernel,
        shape((2 * quarter, hidden_size), BF),
        [SMEM] * 2 + [VMEM] * 2,
        (gate_scales, up_scales, gate_codes, up_codes),
        grant=WIDE,
        flops=2 * quarter * hidden_size,
        nbytes=8 * quarter * hidden_size,
    )
    w_prev = turn(w_own, 1)
    send, one_hot = call(
        slot_kernel,
        (shape((experts * out_chunks, LANES), BF), shape((slots, count), BF)),
        [SMEM, VMEM, VMEM, VMEM, VMEM],
        (live_tokens, routes_t, weights_t, tokens, grad_out),
        flops=2 * slots * count * quarter * 4,
        nbytes=2 * slots * 2 * quarter,
        scratch=[pltpu.VMEM((experts * out_chunks, LANES), F32)],
    )
    got = lax.all_to_all(
        send.reshape(experts, out_chunks, LANES), "expert", split_axis=0, concat_axis=0, tiled=True
    )
    w_next = turn(w_own, -1)
    w_far = turn(w_prev, 1)
    w_down = call(
        dequant_one_kernel,
        shape(down_codes.shape, BF),
        [SMEM, VMEM],
        (down_scales, down_codes),
        flops=quarter * hidden_size,
        nbytes=4 * quarter * hidden_size,
    )
    part, rows = call(
        row_kernel,
        (shape((parts, span, quarter + hidden_size), BF), shape((slots, 2 * quarter), BF)),
        [VMEM] * 2,
        (got.reshape(experts * out_chunks, LANES), w_down),
        flops=2 * slots * quarter * hidden_size,
        nbytes=8 * slots * hidden_size,
        scratch=[pltpu.VMEM((experts * out_chunks, LANES), F32)],
    )
    part = lax.all_to_all(part, "dp", split_axis=0, concat_axis=0, tiled=True)
    grad, acts = call(
        act_kernel,
        (shape((parts, span, quarter + LANES), BF), shape((3 * span, hidden_size), BF)),
        [SMEM] + [VMEM] * 5,
        (me.reshape(1), part, w_own, w_next, w_far, w_prev),
        flops=8 * slots * quarter * hidden_size,
        nbytes=16 * quarter * hidden_size,
    )
    grad = lax.all_to_all(grad, "dp", split_axis=0, concat_axis=0, tiled=True)
    ret = call(
        pack_kernel,
        shape((experts * back_chunks, LANES), BF),
        [VMEM],
        (grad.reshape(slots, quarter + LANES),),
        nbytes=8 * slots * quarter,
        scratch=[pltpu.VMEM((experts * back_chunks, LANES), F32)],
    )
    ret, acts = lax.optimization_barrier((ret, acts))
    ret = lax.all_to_all(
        ret.reshape(experts, back_chunks, LANES), "expert", split_axis=0, concat_axis=0, tiled=True
    )
    grad_gate, grad_up, grad_down = call(
        weight_grad_kernel,
        (
            shape((quarter, hidden_size), BF),
            shape((quarter, hidden_size), BF),
            shape((hidden_size, quarter), BF),
        ),
        [SMEM] + [VMEM] * 5,
        (me.reshape(1), rows, acts, turn(acts, 1), turn(acts, 2), turn(acts, 3)),
        flops=6 * slots * quarter * hidden_size,
        nbytes=16 * slots * hidden_size,
    )
    grad_tokens, grad_weights_t = call(
        home_kernel,
        (shape((count, quarter), BF), shape((2, count), F32)),
        [VMEM] * 4,
        (routes_t, weights_t, one_hot, ret.reshape(experts * back_chunks, LANES)),
        flops=2 * slots * count * quarter,
        nbytes=2 * slots * quarter,
        scratch=[pltpu.VMEM((experts * back_chunks, LANES), F32)],
    )
    return (grad_tokens, grad_weights_t.T, grad_gate, grad_up, grad_down)


def solution(mesh):
    placed = (
        P("expert", "dp"),
        P("expert", None),
        P("expert", None),
        P("expert"),
        P("dp", "expert"),
        P("dp", "expert"),
        P("dp", "expert"),
        P("dp", "expert"),
        P("expert", "dp"),
        P("expert", "dp"),
        P("expert", "dp"),
    )
    return jax.shard_map(
        layer,
        mesh=mesh,
        in_specs=placed,
        out_specs=(
            P("expert", "dp"),
            P("expert", None),
            P("dp", "expert"),
            P("dp", "expert"),
            P("expert", "dp"),
        ),
        check_vma=False,
    )
```

time: 166 us -> 187 us (1.13)
  waiting for transfers between devices: 60.6 us -> 93.6 us
  blocking collectives: 41.9 us -> 9.28 us
  starting transfers between devices: 40.9 us -> 60.8 us
  Pallas kernels: 10 us -> 16.5 us
  local copies, waits for them, and re-layouts: 10.4 us -> 5.1 us
    ppermute x3 -> x6, waiting for transfers between devices: 5.2 us -> 80.3 us  [turn(): lax.ppermute(value, 'dp', [(i, (i + shift) % parts) for i in range(parts)])]
    all_to_all x2 -> x3, waiting for transfers between devices: 55.4 us -> 13.3 us  [the longest x1 10.2 us: layer(): part = lax.all_to_all(part, 'dp', split_axis=0, concat_axis=0, tiled=True)]
    all_to_all x2 -> x1, blocking collectives: 41.9 us -> 9.28 us  [layer(): grad = lax.all_to_all(grad, 'dp', split_axis=0, concat_axis=0, tiled=True)]
    all_to_all x2 -> x3, starting transfers between devices: 32.5 us -> 44.5 us  [the longest x1 20.4 us: layer(): lax.all_to_all(send.reshape(experts, out_chunks, LANES), 'expert', split_...]
    ppermute x3 -> x6, starting transfers between devices: 8.43 us -> 16.3 us  [turn(): lax.ppermute(value, 'dp', [(i, (i + shift) % parts) for i in range(parts)])]
    pallas_call x7 -> x8, Pallas kernels: 10 us -> 16.5 us  [call(): pl.pallas_call(kernel, out_shape=outs, in_specs=in_specs, out_specs=jax.t...]
    unnamed x39 -> x25, local copies, waits for them, and re-layouts: 10.4 us -> 5.1 us
  transfers between devices with their start and end apart: 5 -> 9, of which waited for: 4 -> 7; matrix products, arithmetic and copies ran while one was open for 0% -> 0% of each run, Pallas kernels for 2% -> 4%
where the time goes in v3:
time: 187 us
  waiting for transfers between devices  93.6 us (50%)
  starting transfers between devices  60.8 us (33%)
  Pallas kernels  16.5 us (9%)
  blocking collectives  9.28 us (5%)
  local copies, waits for them, and re-layouts  5.1 us (3%)
    ppermute x6, waiting for transfers between devices, turn(): lax.ppermute(value, 'dp', [(i, (i + shift) % parts) for i in range(parts)])  80.3 us
    all_to_all x1, starting transfers between devices, layer(): lax.all_to_all(send.reshape(experts, out_chunks, LANES), 'expert', split_...  20.4 us
    all_to_all x1, starting transfers between devices, layer(): lax.all_to_all(ret.reshape(experts, back_chunks, LANES), 'expert', split_...  20.2 us
    pallas_call x8, Pallas kernels, call(): pl.pallas_call(kernel, out_shape=outs, in_specs=in_specs, out_specs=jax.t...  16.5 us
    ppermute x6, starting transfers between devices, turn(): lax.ppermute(value, 'dp', [(i, (i + shift) % parts) for i in range(parts)])  16.3 us
    all_to_all x1, waiting for transfers between devices, layer(): part = lax.all_to_all(part, 'dp', split_axis=0, concat_axis=0, tiled=True)  10.2 us
    all_to_all x1, blocking collectives, layer(): grad = lax.all_to_all(grad, 'dp', split_axis=0, concat_axis=0, tiled=True)  9.28 us
    unnamed x25, local copies, waits for them, and re-layouts  5.1 us
  transfers between devices with their start and end apart: 9, of which 7 were waited for; matrix products, arithmetic and copies ran while one was open for 0% of the time, Pallas kernels for 4%

profile of v3, /device:TPU:1, one launch (start us, length us, event | category | flops | bytes accessed | tf_op | source)
XLA Modules:
  0.0 186.7 jit_solution(3492288986530114392)
XLA Ops:
  1.3 0.0 copy-start.3
  1.3 0.7 copy-done.3
  2.0 0.0 copy-start.5
  2.0 0.7 copy-done.5
  2.6 0.0 copy-start.9
  2.6 0.9 copy-done.9
  3.5 0.9 copy-done.10
  4.4 1.7 shard_map.146
  6.1 20.4 %all-to-all-start = ((bf16[128,24,128]{2,1,0:T(8,128)(2,1)}), bf16[128,24,128]{2,1,0:T(8,128)(2,1)S(1)}, u32[]{:S(2)}, u32[]{:S(2)}) async-start(bf16[128,24,128]{2,1,0:T(8,128)(2,1)} %bitcast.3), calls=%async_computation | async-start | bytes 1572864 | tf_op jit(solution)/shard_map/all_to_all | solution.py:278
  26.5 0.0 copy-start.11
  26.5 0.0 copy-start.2
  26.5 2.9 %shard_map.149.own_ref = bf16[1024,768]{1,0:T(8,128)(2,1)} custom-call(f32[4,6]{1,0:T(4,128)} %gs_ref.1, f32[4,6]{1,0:T(4,128)} %us_ref.1, bf16[512,768]{1,0:T(8,128)(2,1)} %gc_ref.1, bf16[512,768]{1,0:T(8,128)(2,1)} %uc_ref.1), custom_call_target="tpu_custom_call" | custom-call | flops 786432 | bytes 3145728 | tf_op jit(solution)/shard_map/pallas_call | solution.py:30
  29.5 3.2 %collective-permute-start.1 = (bf16[1024,768]{1,0:T(8,128)(2,1)}, bf16[1024,768]{1,0:T(8,128)(2,1)}, u32[]{:S(2)}, u32[]{:S(2)}) collective-permute-start(bf16[1024,768]{1,0:T(8,128)(2,1)} %shard_map.149.own_ref), channel_id=1, source_target_pairs={{0,128},{128,256},{256,384},{384,0},{1,129},{129,257},{257,385},{3... | collective-permute-start | bytes 4718600 | tf_op jit(solution)/shard_map/ppermute | solution.py:257
  32.7 3.4 %collective-permute-start = (bf16[1024,768]{1,0:T(8,128)(2,1)}, bf16[1024,768]{1,0:T(8,128)(2,1)}, u32[]{:S(2)}, u32[]{:S(2)}) collective-permute-start(bf16[1024,768]{1,0:T(8,128)(2,1)} %shard_map.149.own_ref), channel_id=1, source_target_pairs={{0,384},{128,0},{256,128},{384,256},{1,385},{129,1},{257,129},{385... | collective-permute-start | bytes 4718600 | tf_op jit(solution)/shard_map/ppermute | solution.py:257
  36.0 32.0 %collective-permute-done.1.prev_ref = bf16[1024,768]{1,0:T(8,128)(2,1)} collective-permute-done((bf16[1024,768]{1,0:T(8,128)(2,1)}, bf16[1024,768]{1,0:T(8,128)(2,1)}, u32[]{:S(2)}, u32[]{:S(2)}) %collective-permute-start.1) | collective-permute-done | bytes 1572896 | tf_op jit(solution)/shard_map/ppermute | solution.py:257
  68.1 1.9 %collective-permute-start.2 = (bf16[1024,768]{1,0:T(8,128)(2,1)}, bf16[1024,768]{1,0:T(8,128)(2,1)}, u32[]{:S(2)}, u32[]{:S(2)}) collective-permute-start(bf16[1024,768]{1,0:T(8,128)(2,1)} %collective-permute-done.1.prev_ref), channel_id=1, source_target_pairs={{0,128},{128,256},{256,384},{384,0},{1,129},{129,257},{257,385},{3... | collective-permute-start | bytes 4718600 | tf_op jit(solution)/shard_map/ppermute | solution.py:257
  70.0 0.0 copy-done.11
  70.0 0.1 copy.16.ds_ref
  70.1 0.0 copy-done.2
  70.1 0.8 shard_map.147.wd_ref
  70.9 0.0 all-to-all-done
  70.9 0.0 copy-start
  70.9 0.8 shard_map.148
  71.7 0.0 copy-start.1
  71.7 0.9 copy-done.1
  72.7 0.9 copy-done.7
  73.5 3.9 %all-to-all-start.1 = ((bf16[4,96,1280]{2,1,0:T(8,128)(2,1)}), bf16[4,96,1280]{2,1,0:T(8,128)(2,1)S(1)}, u32[]{:S(2)}, u32[]{:S(2)}) async-start(bf16[4,96,1280]{2,1,0:T(8,128)(2,1)} %copy-done.1), calls=%async_computation.1 | async-start | bytes 1966080 | tf_op jit(solution)/shard_map/all_to_all | solution.py:300
  77.5 0.0 collective-permute-done.next_ref
  77.5 28.3 %collective-permute-done.2.far_ref = bf16[1024,768]{1,0:T(8,128)(2,1)} collective-permute-done((bf16[1024,768]{1,0:T(8,128)(2,1)}, bf16[1024,768]{1,0:T(8,128)(2,1)}, u32[]{:S(2)}, u32[]{:S(2)}) %collective-permute-start.2) | collective-permute-done | bytes 1572896 | tf_op jit(solution)/shard_map/ppermute | solution.py:257
  105.8 10.2 %all-to-all-done.1.part_ref = bf16[4,96,1280]{2,1,0:T(8,128)(2,1)S(1)} async-done(((bf16[4,96,1280]{2,1,0:T(8,128)(2,1)}), bf16[4,96,1280]{2,1,0:T(8,128)(2,1)S(1)}, u32[]{:S(2)}, u32[]{:S(2)}) %all-to-all-start.1) | async-done | bytes 983072 | tf_op jit(solution)/shard_map/all_to_all | solution.py:300
  116.0 0.0 copy-done
  116.0 5.4 %shard_map.150 = (bf16[4,96,640]{2,1,0:T(8,128)(2,1)S(1)}, bf16[288,768]{1,0:T(8,128)(2,1)S(1)}) custom-call(s32[1]{0:T(128)} %bitcast.2.me_ref, bf16[4,96,1280]{2,1,0:T(8,128)(2,1)S(1)} %all-to-all-done.1.part_ref, bf16[1024,768]{1,0:T(8,128)(2,1)S(1)} %copy-done, bf16[1024,768]{1,0:T(8,128)(2,1)} %collective-permute-done.next_ref, ...), custom_call_target="tpu_custom_call" | custom-call | flops 1207959552 | bytes 6291456 | tf_op jit(solution)/shard_map/pallas_call | solution.py:30
  121.4 0.0 copy-start.8
  121.5 9.3 %all_to_all.20 = bf16[4,96,640]{2,1,0:T(8,128)(2,1)S(1)} all-to-all(bf16[4,96,640]{2,1,0:T(8,128)(2,1)S(1)} %get-tuple-element.21), channel_id=1, replica_groups=mesh['dp'=4,'expert'=128] {'dp'}, dimensions={0} | all-to-all | bytes 983040 | tf_op jit(solution)/shard_map/all_to_all | solution.py:309
  130.7 1.4 shard_map.151
  132.1 20.2 %all-to-all-start.3 = ((bf16[128,16,128]{2,1,0:T(8,128)(2,1)}), bf16[128,16,128]{2,1,0:T(8,128)(2,1)S(1)}, u32[]{:S(2)}, u32[]{:S(2)}) async-start(bf16[128,16,128]{2,1,0:T(8,128)(2,1)} %bitcast.6), calls=%async_computation.3 | async-start | bytes 1048576 | tf_op jit(solution)/shard_map/all_to_all | solution.py:319
  152.3 2.8 %collective-permute-start.5 = (bf16[288,768]{1,0:T(8,128)(2,1)S(1)}, bf16[288,768]{1,0:T(8,128)(2,1)S(1)}, u32[]{:S(2)}, u32[]{:S(2)}) collective-permute-start(bf16[288,768]{1,0:T(8,128)(2,1)S(1)} %get-tuple-element.27.a0_ref), channel_id=1, source_target_pairs={{0,384},{128,0},{256,128},{384,256},{1,385},{129,1},{257,129},{385... | collective-permute-start | bytes 1327112 | tf_op jit(solution)/shard_map/ppermute | solution.py:257
  155.1 3.1 %collective-permute-start.4 = (bf16[288,768]{1,0:T(8,128)(2,1)S(1)}, bf16[288,768]{1,0:T(8,128)(2,1)S(1)}, u32[]{:S(2)}, u32[]{:S(2)}) collective-permute-start(bf16[288,768]{1,0:T(8,128)(2,1)S(1)} %get-tuple-element.27.a0_ref), channel_id=1, source_target_pairs={{0,256},{128,384},{256,0},{384,128},{1,257},{129,385},{257,1},{385... | collective-permute-start | bytes 1327112 | tf_op jit(solution)/shard_map/ppermute | solution.py:257
  158.2 1.9 %collective-permute-start.3 = (bf16[288,768]{1,0:T(8,128)(2,1)S(1)}, bf16[288,768]{1,0:T(8,128)(2,1)S(1)}, u32[]{:S(2)}, u32[]{:S(2)}) collective-permute-start(bf16[288,768]{1,0:T(8,128)(2,1)S(1)} %get-tuple-element.27.a0_ref), channel_id=1, source_target_pairs={{0,128},{128,256},{256,384},{384,0},{1,129},{129,257},{257,385},{3... | collective-permute-start | bytes 1327112 | tf_op jit(solution)/shard_map/ppermute | solution.py:257
  160.1 4.9 %collective-permute-done.5.a3_ref = bf16[288,768]{1,0:T(8,128)(2,1)S(1)} collective-permute-done((bf16[288,768]{1,0:T(8,128)(2,1)S(1)}, bf16[288,768]{1,0:T(8,128)(2,1)S(1)}, u32[]{:S(2)}, u32[]{:S(2)}) %collective-permute-start.5) | collective-permute-done | bytes 442400 | tf_op jit(solution)/shard_map/ppermute | solution.py:257
  165.0 4.1 %collective-permute-done.4.a2_ref = bf16[288,768]{1,0:T(8,128)(2,1)S(1)} collective-permute-done((bf16[288,768]{1,0:T(8,128)(2,1)S(1)}, bf16[288,768]{1,0:T(8,128)(2,1)S(1)}, u32[]{:S(2)}, u32[]{:S(2)}) %collective-permute-start.4) | collective-permute-done | bytes 442400 | tf_op jit(solution)/shard_map/ppermute | solution.py:257
  169.1 11.0 %collective-permute-done.3.a1_ref = bf16[288,768]{1,0:T(8,128)(2,1)S(1)} collective-permute-done((bf16[288,768]{1,0:T(8,128)(2,1)S(1)}, bf16[288,768]{1,0:T(8,128)(2,1)S(1)}, u32[]{:S(2)}, u32[]{:S(2)}) %collective-permute-start.3) | collective-permute-done | bytes 442400 | tf_op jit(solution)/shard_map/ppermute | solution.py:257
  180.1 0.0 copy-done.8
  180.1 2.3 %shard_map.153 = (bf16[512,768]{1,0:T(8,128)(2,1)}, bf16[512,768]{1,0:T(8,128)(2,1)}, bf16[768,512]{1,0:T(8,128)(2,1)}) custom-call(s32[1]{0:T(128)} %bitcast.2.me_ref, bf16[384,1024]{1,0:T(8,128)(2,1)S(1)} %copy-done.8, bf16[288,768]{1,0:T(8,128)(2,1)S(1)} %get-tuple-element.27.a0_ref, bf16[288,768]{1,0:T(8,128)(2,1)S(1)} %collective-permute-done.3.a1_ref, ...), custom_call_target="tpu_custom_call" | custom-call | flops 905969664 | bytes 4718592 | tf_op jit(solution)/shard_map/pallas_call | solution.py:30
  182.4 3.1 %all-to-all-done.3 = bf16[128,16,128]{2,1,0:T(8,128)(2,1)S(1)} async-done(((bf16[128,16,128]{2,1,0:T(8,128)(2,1)}), bf16[128,16,128]{2,1,0:T(8,128)(2,1)S(1)}, u32[]{:S(2)}, u32[]{:S(2)}) %all-to-all-start.3) | async-done | bytes 524320 | tf_op jit(solution)/shard_map/all_to_all | solution.py:319
  185.5 0.0 copy-done.4
  185.5 0.0 copy-done.6
  185.5 1.2 shard_map.152
  (4 shorter events, 0.0 us)
Async XLA Ops:
  1.3 0.7 copy-start.3
  2.0 0.7 copy-start.5
  2.6 0.9 copy-start.9
  3.5 0.9 copy-start.10
  6.1 64.8 %all-to-all-start = ((bf16[128,24,128]{2,1,0:T(8,128)(2,1)}), bf16[128,24,128]{2,1,0:T(8,128)(2,1)S(1)}, u32[]{:S(2)}, u32[]{:S(2)}) async-start(bf16[128,24,128]{2,1,0:T(8,128)(2,1)} %bitcast.3), calls=%async_computation | async-start | bytes 1572864 | tf_op jit(solution)/shard_map/all_to_all | solution.py:278
  26.5 43.5 %copy-start.11 = (f32[6,4]{0,1:T(4,128)S(1)}, f32[6,4]{0,1:T(4,128)}, u32[]{:S(2)}) copy-start(f32[6,4]{0,1:T(4,128)} %param.20) | copy-start | bytes 292
  26.5 43.6 %copy-start.2 = (bf16[768,512]{1,0:T(8,128)(2,1)S(1)}, bf16[768,512]{1,0:T(8,128)(2,1)}, u32[]{:S(2)}) copy-start(bf16[768,512]{1,0:T(8,128)(2,1)} %dc_ref.1) | copy-start | bytes 2359300
  29.5 38.6 %collective-permute-start.1 = (bf16[1024,768]{1,0:T(8,128)(2,1)}, bf16[1024,768]{1,0:T(8,128)(2,1)}, u32[]{:S(2)}, u32[]{:S(2)}) collective-permute-start(bf16[1024,768]{1,0:T(8,128)(2,1)} %shard_map.149.own_ref), channel_id=1, source_target_pairs={{0,128},{128,256},{256,384},{384,0},{1,129},{129,257},{257,385},{3... | collective-permute-start | bytes 4718600 | tf_op jit(solution)/shard_map/ppermute | solution.py:257
  32.7 44.8 %collective-permute-start = (bf16[1024,768]{1,0:T(8,128)(2,1)}, bf16[1024,768]{1,0:T(8,128)(2,1)}, u32[]{:S(2)}, u32[]{:S(2)}) collective-permute-start(bf16[1024,768]{1,0:T(8,128)(2,1)} %shard_map.149.own_ref), channel_id=1, source_target_pairs={{0,384},{128,0},{256,128},{384,256},{1,385},{129,1},{257,129},{385... | collective-permute-start | bytes 4718600 | tf_op jit(solution)/shard_map/ppermute | solution.py:257
  68.1 37.7 %collective-permute-start.2 = (bf16[1024,768]{1,0:T(8,128)(2,1)}, bf16[1024,768]{1,0:T(8,128)(2,1)}, u32[]{:S(2)}, u32[]{:S(2)}) collective-permute-start(bf16[1024,768]{1,0:T(8,128)(2,1)} %collective-permute-done.1.prev_ref), channel_id=1, source_target_pairs={{0,128},{128,256},{256,384},{384,0},{1,129},{129,257},{257,385},{3... | collective-permute-start | bytes 4718600 | tf_op jit(solution)/shard_map/ppermute | solution.py:257
  70.9 45.1 %copy-start = (bf16[1024,768]{1,0:T(8,128)(2,1)S(1)}, bf16[1024,768]{1,0:T(8,128)(2,1)}, u32[]{:S(2)}) copy-start(bf16[1024,768]{1,0:T(8,128)(2,1)} %shard_map.149.own_ref) | copy-start | bytes 4718596
  71.7 0.9 copy-start.1
  72.7 0.9 copy-start.7
  73.5 42.5 %all-to-all-start.1 = ((bf16[4,96,1280]{2,1,0:T(8,128)(2,1)}), bf16[4,96,1280]{2,1,0:T(8,128)(2,1)S(1)}, u32[]{:S(2)}, u32[]{:S(2)}) async-start(bf16[4,96,1280]{2,1,0:T(8,128)(2,1)} %copy-done.1), calls=%async_computation.1 | async-start | bytes 1966080 | tf_op jit(solution)/shard_map/all_to_all | solution.py:300
  121.4 58.6 %copy-start.8 = (bf16[384,1024]{1,0:T(8,128)(2,1)S(1)}, bf16[384,1024]{1,0:T(8,128)(2,1)}, u32[]{:S(2)}) copy-start(bf16[384,1024]{1,0:T(8,128)(2,1)} %copy-done.7) | copy-start | bytes 2359300
  132.1 53.4 %all-to-all-start.3 = ((bf16[128,16,128]{2,1,0:T(8,128)(2,1)}), bf16[128,16,128]{2,1,0:T(8,128)(2,1)S(1)}, u32[]{:S(2)}, u32[]{:S(2)}) async-start(bf16[128,16,128]{2,1,0:T(8,128)(2,1)} %bitcast.6), calls=%async_computation.3 | async-start | bytes 1048576 | tf_op jit(solution)/shard_map/all_to_all | solution.py:319
  152.3 12.7 %collective-permute-start.5 = (bf16[288,768]{1,0:T(8,128)(2,1)S(1)}, bf16[288,768]{1,0:T(8,128)(2,1)S(1)}, u32[]{:S(2)}, u32[]{:S(2)}) collective-permute-start(bf16[288,768]{1,0:T(8,128)(2,1)S(1)} %get-tuple-element.27.a0_ref), channel_id=1, source_target_pairs={{0,384},{128,0},{256,128},{384,256},{1,385},{129,1},{257,129},{385... | collective-permute-start | bytes 1327112 | tf_op jit(solution)/shard_map/ppermute | solution.py:257
  155.1 14.0 %collective-permute-start.4 = (bf16[288,768]{1,0:T(8,128)(2,1)S(1)}, bf16[288,768]{1,0:T(8,128)(2,1)S(1)}, u32[]{:S(2)}, u32[]{:S(2)}) collective-permute-start(bf16[288,768]{1,0:T(8,128)(2,1)S(1)} %get-tuple-element.27.a0_ref), channel_id=1, source_target_pairs={{0,256},{128,384},{256,0},{384,128},{1,257},{129,385},{257,1},{385... | collective-permute-start | bytes 1327112 | tf_op jit(solution)/shard_map/ppermute | solution.py:257
  158.2 21.9 %collective-permute-start.3 = (bf16[288,768]{1,0:T(8,128)(2,1)S(1)}, bf16[288,768]{1,0:T(8,128)(2,1)S(1)}, u32[]{:S(2)}, u32[]{:S(2)}) collective-permute-start(bf16[288,768]{1,0:T(8,128)(2,1)S(1)} %get-tuple-element.27.a0_ref), channel_id=1, source_target_pairs={{0,128},{128,256},{256,384},{384,0},{1,129},{129,257},{257,385},{3... | collective-permute-start | bytes 1327112 | tf_op jit(solution)/shard_map/ppermute | solution.py:257
  180.1 5.4 %copy-start.4 = (s32[128,2]{0,1:T(2,128)S(1)}, s32[128,2]{0,1:T(2,128)}, u32[]{:S(2)}) copy-start(s32[128,2]{0,1:T(2,128)} %param.12) | copy-start | bytes 3076
  180.1 5.4 %copy-start.6 = (f32[128,2]{0,1:T(2,128)S(1)}, f32[128,2]{0,1:T(2,128)}, u32[]{:S(2)}) copy-start(f32[128,2]{0,1:T(2,128)} %param.13) | copy-start | bytes 3076

commit v4 on v3

--- a/solution.py
+++ b/solution.py
@@ -10,12 +10,14 @@
 F32 = jnp.float32
 CAP = 3
 LANES = 128
-GRANT = 24 << 20
-WIDE = 60 << 20
+GRANT = 62 << 20
+MIDDLE = 50 << 20
+SMALL = 24 << 20
 LAST = (((1,), (1,)), ((), ()))
 FIRST = (((0,), (0,)), ((), ()))
 VMEM = pl.BlockSpec(memory_space=pltpu.VMEM)
 SMEM = pl.BlockSpec(memory_space=pltpu.SMEM)
+ANY = pl.BlockSpec(memory_space=pl.ANY)
 
 
 def split3(v):
@@ -26,12 +28,12 @@
     return hi, mid, lo
 
 
-def call(kernel, outs, in_specs, args, flops=0, nbytes=0, scratch=(), grant=GRANT):
+def call(kernel, outs, in_specs, args, flops=0, nbytes=0, scratch=(), grant=GRANT, place=VMEM):
     return pl.pallas_call(
         kernel,
         out_shape=outs,
         in_specs=in_specs,
-        out_specs=jax.tree.map(lambda _: VMEM, outs),
+        out_specs=jax.tree.map(lambda _: place, outs),
         scratch_shapes=scratch,
         compiler_params=pltpu.CompilerParams(vmem_limit_bytes=grant),
         cost_estimate=pl.CostEstimate(flops=flops, bytes_accessed=nbytes, transcendentals=0),
@@ -88,53 +90,83 @@
     dequant(ds_ref, dc_ref, out_ref, 0)
 
 
-def row_kernel(got_ref, wd_ref, out_ref, rows_ref, mix_ref):
+def row_kernel(got_hbm, wd_hbm, out_hbm, rows_hbm, got_ref, wd_ref, out_ref, rows_ref, mix_ref, sems):
     parts, span, _ = out_ref.shape
     quarter = rows_ref.shape[1] // 2
     groups = rows_ref.shape[0] // CAP
+    near = groups // parts
     wide = quarter // LANES
     chunks = 2 * CAP * wide
+    load = [
+        pltpu.make_async_copy(got_hbm, got_ref, sems.at[0]),
+        pltpu.make_async_copy(wd_hbm, wd_ref, sems.at[1]),
+    ]
+    for copy in load:
+        copy.start()
+    load[0].wait()
     mix_ref[...] = got_ref[...].astype(F32)
     for kind in range(2):
         for p in range(CAP):
             for h in range(wide):
                 at = (kind * CAP + p) * wide + h
                 lane = kind * quarter + h * LANES
-                rows_ref[p * groups : (p + 1) * groups, lane : lane + LANES] = mix_ref[
-                    pl.ds(at, groups, stride=chunks), :
-                ].astype(BF)
+                value = mix_ref[pl.ds(at, groups, stride=chunks), :].astype(BF)
+                for j in range(parts):
+                    line = j * span + p * near
+                    piece = value[j * near : (j + 1) * near]
+                    rows_ref[line : line + near, lane : lane + LANES] = piece
+                    if kind == 0:
+                        out_ref[j, p * near : (p + 1) * near, lane : lane + LANES] = piece
+    save = [pltpu.make_async_copy(rows_ref, rows_hbm, sems.at[2])]
+    save[0].start()
+    load[1].wait()
     back = lax.dot_general(
         rows_ref[:, quarter:], wd_ref[...], LAST, preferred_element_type=F32
     ).astype(BF)
     for j in range(parts):
-        lines = slice(j * span, (j + 1) * span)
-        out_ref[j, :, :quarter] = rows_ref[lines, :quarter]
-        out_ref[j, :, quarter:] = back[lines]
-
-
-def act_kernel(me_ref, part_ref, own_ref, next_ref, far_ref, prev_ref, out_ref, act_ref):
+        out_ref[j, :, quarter:] = back[j * span : (j + 1) * span]
+        copy = pltpu.make_async_copy(out_ref.at[j], out_hbm.at[j], sems.at[3 + j])
+        copy.start()
+        save.append(copy)
+    for copy in save:
+        copy.wait()
+
+
+def act_kernel(
+    me_ref, part_ref, own_hbm, next_hbm, far_gate_hbm, far_up_hbm, prev_hbm, out_ref, act_ref, w_ref, mix_ref, sems
+):
     parts, span, _ = part_ref.shape
-    quarter = own_ref.shape[0] // 2
+    near = span // CAP
+    quarter = w_ref.shape[1] // 2
+    wide = quarter // LANES
+    chunks = out_ref.shape[1] // near
     owners = [lax.rem(me_ref[0] + shift, parts) for shift in range(parts)]
-
-    blocks = (own_ref, next_ref, far_ref, prev_ref)
-
-    def gate_of(shift):
-        return blocks[shift][:quarter, :]
-
-    def up_of(shift):
-        return blocks[shift][quarter:, :]
-
-    gate_pre = up_pre = 0.0
-    for shift in range(parts):
-        token_rows = part_ref[owners[shift], :, :quarter]
-        gate = jnp.dot(token_rows, gate_of(shift), preferred_element_type=F32)
-        gate_pre = gate_pre + gate.astype(BF).astype(F32)
-        up = jnp.dot(token_rows, up_of(shift), preferred_element_type=F32)
-        up_pre = up_pre + up.astype(BF).astype(F32)
+    copies = [
+        pltpu.make_async_copy(source, target, sems.at[n])
+        for n, (source, target) in enumerate(
+            (
+                (own_hbm, w_ref.at[0]),
+                (next_hbm, w_ref.at[1]),
+                (prev_hbm, w_ref.at[3]),
+                (far_gate_hbm, w_ref.at[2, :quarter]),
+                (far_up_hbm, w_ref.at[2, quarter:]),
+            )
+        )
+    ]
+    for copy in copies:
+        copy.start()
     grad_hidden = part_ref[0, :, quarter:].astype(F32)
     for j in range(1, parts):
         grad_hidden = grad_hidden + part_ref[j, :, quarter:].astype(F32)
+    gate_pre = up_pre = 0.0
+    for shift, needed in ((0, (0,)), (1, (1,)), (3, (2,)), (2, (3, 4))):
+        for n in needed:
+            copies[n].wait()
+        token_rows = part_ref[owners[shift], :, :quarter]
+        gate = jnp.dot(token_rows, w_ref[shift, :quarter, :], preferred_element_type=F32)
+        gate_pre = gate_pre + gate.astype(BF).astype(F32)
+        up = jnp.dot(token_rows, w_ref[shift, quarter:, :], preferred_element_type=F32)
+        up_pre = up_pre + up.astype(BF).astype(F32)
     sig = jax.nn.sigmoid(gate_pre)
     activated = gate_pre * sig
     hidden = (activated * up_pre).astype(BF)
@@ -146,29 +178,24 @@
     score = jnp.sum(hidden.astype(F32) * grad_hidden, axis=1, keepdims=True)
     lane = lax.broadcasted_iota(jnp.int32, (span, LANES), 1)
     hi, mid, lo = (v.astype(F32) for v in split3(score))
-    scores = jnp.where(
-        lane == 0, hi, jnp.where(lane == 1, mid, jnp.where(lane == 2, lo, 0.0))
-    ).astype(BF)
+    scores = jnp.where(lane == 0, hi, jnp.where(lane == 1, mid, jnp.where(lane == 2, lo, 0.0)))
+    for p in range(CAP):
+        mix_ref[pl.ds(CAP * wide + p, near, stride=chunks), :] = scores[p * near : (p + 1) * near]
+    for c in range(CAP * wide + CAP, chunks):
+        mix_ref[pl.ds(c, near, stride=chunks), :] = jnp.zeros((near, LANES), F32)
     for shift in range(parts):
-        grad = lax.dot_general(gate_delta, gate_of(shift), LAST, preferred_element_type=F32)
-        grad = grad + lax.dot_general(up_delta, up_of(shift), LAST, preferred_element_type=F32)
-        out_ref[owners[shift], :, :quarter] = grad.astype(BF)
-        out_ref[owners[shift], :, quarter:] = scores
-
-
-def pack_kernel(grad_ref, out_ref, mix_ref):
-    groups = grad_ref.shape[0] // CAP
-    wide = grad_ref.shape[1] // LANES - 1
-    chunks = out_ref.shape[0] // groups
-    for p in range(CAP):
-        for h in range(wide + 1):
-            at = p * wide + h if h < wide else CAP * wide + p
-            mix_ref[pl.ds(at, groups, stride=chunks), :] = grad_ref[
-                p * groups : (p + 1) * groups, h * LANES : (h + 1) * LANES
-            ].astype(F32)
-    for c in range(CAP * wide + CAP, chunks):
-        mix_ref[pl.ds(c, groups, stride=chunks), :] = jnp.zeros((groups, LANES), F32)
-    out_ref[...] = mix_ref[...].astype(BF)
+        grad = lax.dot_general(
+            gate_delta, w_ref[shift, :quarter, :], LAST, preferred_element_type=F32
+        )
+        grad = grad + lax.dot_general(
+            up_delta, w_ref[shift, quarter:, :], LAST, preferred_element_type=F32
+        )
+        for p in range(CAP):
+            for h in range(wide):
+                mix_ref[pl.ds(p * wide + h, near, stride=chunks), :] = grad[
+                    p * near : (p + 1) * near, h * LANES : (h + 1) * LANES
+                ]
+        out_ref[owners[shift]] = mix_ref[...].astype(BF)
 
 
 def weight_grad_kernel(me_ref, rows_ref, a0_ref, a1_ref, a2_ref, a3_ref, gg_ref, gu_ref, gd_ref):
@@ -261,11 +288,11 @@
         shape((2 * quarter, hidden_size), BF),
         [SMEM] * 2 + [VMEM] * 2,
         (gate_scales, up_scales, gate_codes, up_codes),
-        grant=WIDE,
         flops=2 * quarter * hidden_size,
         nbytes=8 * quarter * hidden_size,
     )
     w_prev = turn(w_own, 1)
+    w_next = turn(w_own, -1)
     send, one_hot = call(
         slot_kernel,
         (shape((experts * out_chunks, LANES), BF), shape((slots, count), BF)),
@@ -278,8 +305,8 @@
     got = lax.all_to_all(
         send.reshape(experts, out_chunks, LANES), "expert", split_axis=0, concat_axis=0, tiled=True
     )
-    w_next = turn(w_own, -1)
-    w_far = turn(w_prev, 1)
+    far_gate = turn(w_next[:quarter], -1)
+    far_up = turn(w_prev[quarter:], 1)
     w_down = call(
         dequant_one_kernel,
         shape(down_codes.shape, BF),
@@ -291,30 +318,39 @@
     part, rows = call(
         row_kernel,
         (shape((parts, span, quarter + hidden_size), BF), shape((slots, 2 * quarter), BF)),
-        [VMEM] * 2,
+        [ANY] * 2,
         (got.reshape(experts * out_chunks, LANES), w_down),
         flops=2 * slots * quarter * hidden_size,
         nbytes=8 * slots * hidden_size,
-        scratch=[pltpu.VMEM((experts * out_chunks, LANES), F32)],
+        scratch=[
+            pltpu.VMEM((experts * out_chunks, LANES), BF),
+            pltpu.VMEM((hidden_size, quarter), BF),
+            pltpu.VMEM((parts, span, quarter + hidden_size), BF),
+            pltpu.VMEM((slots, 2 * quarter), BF),
+            pltpu.VMEM((experts * out_chunks, LANES), F32),
+            pltpu.SemaphoreType.DMA((3 + parts,)),
+        ],
+        place=ANY,
     )
     part = lax.all_to_all(part, "dp", split_axis=0, concat_axis=0, tiled=True)
-    grad, acts = call(
+    ret, acts = call(
         act_kernel,
-        (shape((parts, span, quarter + LANES), BF), shape((3 * span, hidden_size), BF)),
-        [SMEM] + [VMEM] * 5,
-        (me.reshape(1), part, w_own, w_next, w_far, w_prev),
+        (
+            shape((parts, span // CAP * back_chunks, LANES), BF),
+            shape((3 * span, hidden_size), BF),
+        ),
+        [SMEM, VMEM] + [ANY] * 5,
+        (me.reshape(1), part, w_own, w_next, far_gate, far_up, w_prev),
+        grant=MIDDLE,
         flops=8 * slots * quarter * hidden_size,
         nbytes=16 * quarter * hidden_size,
-    )
-    grad = lax.all_to_all(grad, "dp", split_axis=0, concat_axis=0, tiled=True)
-    ret = call(
-        pack_kernel,
-        shape((experts * back_chunks, LANES), BF),
-        [VMEM],
-        (grad.reshape(slots, quarter + LANES),),
-        nbytes=8 * slots * quarter,
-        scratch=[pltpu.VMEM((experts * back_chunks, LANES), F32)],
-    )
+        scratch=[
+            pltpu.VMEM((parts, 2 * quarter, hidden_size), BF),
+            pltpu.VMEM((span // CAP * back_chunks, LANES), F32),
+            pltpu.SemaphoreType.DMA((5,)),
+        ],
+    )
+    ret = lax.all_to_all(ret, "dp", split_axis=0, concat_axis=0, tiled=True)
     ret, acts = lax.optimization_barrier((ret, acts))
     ret = lax.all_to_all(
         ret.reshape(experts, back_chunks, LANES), "expert", split_axis=0, concat_axis=0, tiled=True
@@ -328,6 +364,7 @@
         ),
         [SMEM] + [VMEM] * 5,
         (me.reshape(1), rows, acts, turn(acts, 1), turn(acts, 2), turn(acts, 3)),
+        grant=SMALL,
         flops=6 * slots * quarter * hidden_size,
         nbytes=16 * slots * hidden_size,
     )
@@ -336,6 +373,7 @@
         (shape((count, quarter), BF), shape((2, count), F32)),
         [VMEM] * 4,
         (routes_t, weights_t, one_hot, ret.reshape(experts * back_chunks, LANES)),
+        grant=SMALL,
         flops=2 * slots * count * quarter,
         nbytes=2 * slots * quarter,
         scratch=[pltpu.VMEM((experts * back_chunks, LANES), F32)],

time: 187 us -> 174 us (0.930)
  waiting for transfers between devices: 93.6 us -> 67.9 us
  starting transfers between devices: 60.8 us -> 67.2 us
  blocking collectives: 9.28 us -> 13.5 us
  Pallas kernels: 16.5 us -> 19.5 us
    ppermute x6 -> x7, waiting for transfers between devices: 80.3 us -> 57.8 us  [turn(): lax.ppermute(value, 'dp', [(i, (i + shift) % parts) for i in range(parts)])]
    ppermute x6 -> x7, starting transfers between devices: 16.3 us -> 21 us  [turn(): lax.ppermute(value, 'dp', [(i, (i + shift) % parts) for i in range(parts)])]
    all_to_all x1, blocking collectives: 9.28 us -> 13.5 us  [layer(): ret = lax.all_to_all(ret, 'dp', split_axis=0, concat_axis=0, tiled=True)]
    unnamed x25 -> x15, local copies, waits for them, and re-layouts: 5.1 us -> 1.86 us
    all_to_all x1, waiting for transfers between devices: 10.2 us -> 7.1 us  [layer(): part = lax.all_to_all(part, 'dp', split_axis=0, concat_axis=0, tiled=True)]
    pallas_call x8 -> x7, Pallas kernels: 16.5 us -> 19.5 us  [call(): pl.pallas_call(kernel, out_shape=outs, in_specs=in_specs, out_specs=jax.t...]
    slice x0 -> x2, local copies, waits for them, and re-layouts: none -> 1.95 us  [the longest x1 1.02 us: layer(): far_up = turn(w_prev[quarter:], 1)]
  transfers between devices with their start and end apart: 9 -> 10, of which waited for: 7 -> 8; matrix products, arithmetic and copies ran while one was open for 0% -> 2% of each run, Pallas kernels for 4% -> 6%
where the time goes in v4:
time: 174 us; the launch traced here: 173 us
  waiting for transfers between devices  67.9 us (39%)
  starting transfers between devices  67.2 us (39%)
  Pallas kernels  19.5 us (11%)
  blocking collectives  13.5 us (8%)
  local copies, waits for them, and re-layouts  3.81 us (2%)
    ppermute x7, waiting for transfers between devices, turn(): lax.ppermute(value, 'dp', [(i, (i + shift) % parts) for i in range(parts)])  57.8 us
    all_to_all x1, starting transfers between devices, layer(): lax.all_to_all(ret.reshape(experts, back_chunks, LANES), 'expert', split_...  21.9 us
    ppermute x7, starting transfers between devices, turn(): lax.ppermute(value, 'dp', [(i, (i + shift) % parts) for i in range(parts)])  21 us
    all_to_all x1, starting transfers between devices, layer(): lax.all_to_all(send.reshape(experts, out_chunks, LANES), 'expert', split_...  20.8 us
    pallas_call x7, Pallas kernels, call(): pl.pallas_call(kernel, out_shape=outs, in_specs=in_specs, out_specs=jax.t...  19.5 us
    all_to_all x1, blocking collectives, layer(): ret = lax.all_to_all(ret, 'dp', split_axis=0, concat_axis=0, tiled=True)  13.5 us
    all_to_all x1, waiting for transfers between devices, layer(): part = lax.all_to_all(part, 'dp', split_axis=0, concat_axis=0, tiled=True)  7.1 us
    all_to_all x1, starting transfers between devices, layer(): part = lax.all_to_all(part, 'dp', split_axis=0, concat_axis=0, tiled=True)  3.52 us
  transfers between devices with their start and end apart: 10, of which 8 were waited for; matrix products, arithmetic and copies ran while one was open for 2% of the time, Pallas kernels for 6%

profile of v4, /device:TPU:1, one launch (start us, length us, event | category | flops | bytes accessed | tf_op | source)
XLA Modules:
  0.0 173.3 jit_solution(875443978812892399)
XLA Ops:
  1.3 2.7 %shard_map.146 = (bf16[3072,128]{1,0:T(8,128)(2,1)}, bf16[384,128]{1,0:T(8,128)(2,1)}) custom-call(s32[1]{0:T(128)S(6)} %copy.17.live_ref, s32[2,128]{1,0:T(2,128)} %bitcast.9, f32[2,128]{1,0:T(2,128)} %bitcast.11, bf16[128,512]{1,0:T(8,128)(2,1)} %tokens_ref.1, bf16[128,512]{1,0:T(8,128)(2,1)} %grad_ref.1), custom_call_target="tpu_custom_call" | custom-call | flops 201326592 | bytes 786432 | tf_op jit(solution)/shard_map/pallas_call | solution.py:32
  3.9 20.8 %all-to-all-start = ((bf16[128,24,128]{2,1,0:T(8,128)(2,1)}), bf16[128,24,128]{2,1,0:T(8,128)(2,1)}, u32[]{:S(2)}, u32[]{:S(2)}) async-start(bf16[128,24,128]{2,1,0:T(8,128)(2,1)} %bitcast.13), calls=%async_computation | async-start | bytes 1572864 | tf_op jit(solution)/shard_map/all_to_all | solution.py:305
  24.7 2.9 %shard_map.149.own_hbm = bf16[1024,768]{1,0:T(8,128)(2,1)} custom-call(f32[4,6]{1,0:T(4,128)} %gs_ref.1, f32[4,6]{1,0:T(4,128)} %us_ref.1, bf16[512,768]{1,0:T(8,128)(2,1)} %gc_ref.1, bf16[512,768]{1,0:T(8,128)(2,1)} %uc_ref.1), custom_call_target="tpu_custom_call" | custom-call | flops 786432 | bytes 3145728 | tf_op jit(solution)/shard_map/pallas_call | solution.py:32
  27.6 0.0 copy-start.6
  27.6 3.3 %collective-permute-start.2 = (bf16[1024,768]{1,0:T(8,128)(2,1)}, bf16[1024,768]{1,0:T(8,128)(2,1)S(1)}, u32[]{:S(2)}, u32[]{:S(2)}) collective-permute-start(bf16[1024,768]{1,0:T(8,128)(2,1)} %shard_map.149.own_hbm), channel_id=1, source_target_pairs={{0,128},{128,256},{256,384},{384,0},{1,129},{129,257},{257,385},{3... | collective-permute-start | bytes 4718600 | tf_op jit(solution)/shard_map/ppermute | solution.py:284
  30.9 3.4 %collective-permute-start = (bf16[1024,768]{1,0:T(8,128)(2,1)}, bf16[1024,768]{1,0:T(8,128)(2,1)S(1)}, u32[]{:S(2)}, u32[]{:S(2)}) collective-permute-start(bf16[1024,768]{1,0:T(8,128)(2,1)} %shard_map.149.own_hbm), channel_id=1, source_target_pairs={{0,384},{128,0},{256,128},{384,256},{1,385},{129,1},{257,129},{385... | collective-permute-start | bytes 4718600 | tf_op jit(solution)/shard_map/ppermute | solution.py:284
  34.3 32.0 %collective-permute-done.2.prev_hbm = bf16[1024,768]{1,0:T(8,128)(2,1)S(1)} collective-permute-done((bf16[1024,768]{1,0:T(8,128)(2,1)}, bf16[1024,768]{1,0:T(8,128)(2,1)S(1)}, u32[]{:S(2)}, u32[]{:S(2)}) %collective-permute-start.2) | collective-permute-done | bytes 1572896 | tf_op jit(solution)/shard_map/ppermute | solution.py:284
  66.3 0.0 copy-start.4
  66.3 1.0 slice.9
  67.3 1.9 %collective-permute-start.3 = (bf16[512,768]{1,0:T(8,128)(2,1)}, bf16[512,768]{1,0:T(8,128)(2,1)S(1)}, u32[]{:S(2)}, u32[]{:S(2)}) collective-permute-start(bf16[512,768]{1,0:T(8,128)(2,1)} %slice.9), channel_id=1, source_target_pairs={{0,128},{128,256},{256,384},{384,0},{1,129},{129,257},{257,385},{3... | collective-permute-start | bytes 2359304 | tf_op jit(solution)/shard_map/ppermute | solution.py:284
  69.2 0.0 collective-permute-done.next_hbm
  69.2 0.0 copy-start.5
  69.2 1.2 copy-done.5
  70.4 0.9 slice.8
  71.3 0.0 copy-done.4
  71.3 4.6 %collective-permute-start.1 = (bf16[512,768]{1,0:T(8,128)(2,1)}, bf16[512,768]{1,0:T(8,128)(2,1)S(1)}, u32[]{:S(2)}, u32[]{:S(2)}) collective-permute-start(bf16[512,768]{1,0:T(8,128)(2,1)} %slice.8), channel_id=1, source_target_pairs={{0,384},{128,0},{256,128},{384,256},{1,385},{129,1},{257,129},{385... | collective-permute-start | bytes 2359304 | tf_op jit(solution)/shard_map/ppermute | solution.py:284
  75.9 0.0 copy-done.6
  75.9 0.7 copy.16.ds_ref
  76.6 2.2 %shard_map.147.wd_hbm = bf16[768,512]{1,0:T(8,128)(2,1)} custom-call(f32[6,4]{1,0:T(8,128)} %copy.16.ds_ref, bf16[768,512]{1,0:T(8,128)(2,1)} %dc_ref.1), custom_call_target="tpu_custom_call" | custom-call | flops 393216 | bytes 1572864 | tf_op jit(solution)/shard_map/pallas_call | solution.py:32
  78.7 0.0 all-to-all-done
  78.7 3.0 %shard_map.148 = (bf16[4,96,1280]{2,1,0:T(8,128)(2,1)}, bf16[384,1024]{1,0:T(8,128)(2,1)}) custom-call(bf16[3072,128]{1,0:T(8,128)(2,1)} %bitcast.4.got_hbm, bf16[768,512]{1,0:T(8,128)(2,1)} %shard_map.147.wd_hbm), custom_call_target="tpu_custom_call" | custom-call | flops 301989888 | bytes 2359296 | tf_op jit(solution)/shard_map/pallas_call | solution.py:32
  81.8 3.5 %all-to-all-start.1 = ((bf16[4,96,1280]{2,1,0:T(8,128)(2,1)}), bf16[4,96,1280]{2,1,0:T(8,128)(2,1)S(1)}, u32[]{:S(2)}, u32[]{:S(2)}) async-start(bf16[4,96,1280]{2,1,0:T(8,128)(2,1)} %get-tuple-element.20), calls=%async_computation.1 | async-start | bytes 1966080 | tf_op jit(solution)/shard_map/all_to_all | solution.py:335
  85.3 2.7 %collective-permute-done.3.far_up_hbm = bf16[512,768]{1,0:T(8,128)(2,1)S(1)} collective-permute-done((bf16[512,768]{1,0:T(8,128)(2,1)}, bf16[512,768]{1,0:T(8,128)(2,1)S(1)}, u32[]{:S(2)}, u32[]{:S(2)}) %collective-permute-start.3) | collective-permute-done | bytes 786464 | tf_op jit(solution)/shard_map/ppermute | solution.py:284
  88.0 3.1 %collective-permute-done.1.far_gate_hbm = bf16[512,768]{1,0:T(8,128)(2,1)S(1)} collective-permute-done((bf16[512,768]{1,0:T(8,128)(2,1)}, bf16[512,768]{1,0:T(8,128)(2,1)S(1)}, u32[]{:S(2)}, u32[]{:S(2)}) %collective-permute-start.1) | collective-permute-done | bytes 786464 | tf_op jit(solution)/shard_map/ppermute | solution.py:284
  91.2 7.1 %all-to-all-done.1.part_ref = bf16[4,96,1280]{2,1,0:T(8,128)(2,1)S(1)} async-done(((bf16[4,96,1280]{2,1,0:T(8,128)(2,1)}), bf16[4,96,1280]{2,1,0:T(8,128)(2,1)S(1)}, u32[]{:S(2)}, u32[]{:S(2)}) %all-to-all-start.1) | async-done | bytes 983072 | tf_op jit(solution)/shard_map/all_to_all | solution.py:335
  98.3 5.2 %shard_map.150 = (bf16[4,512,128]{2,1,0:T(8,128)(2,1)S(1)}, bf16[288,768]{1,0:T(8,128)(2,1)S(1)}) custom-call(s32[1]{0:T(128)} %bitcast.2.me_ref, bf16[4,96,1280]{2,1,0:T(8,128)(2,1)S(1)} %all-to-all-done.1.part_ref, bf16[1024,768]{1,0:T(8,128)(2,1)} %shard_map.149.own_hbm, bf16[1024,768]{1,0:T(8,128)(2,1)} %copy-done.5, ...), custom_call_target="tpu_custom_call" | custom-call | flops 1207959552 | bytes 6291456 | tf_op jit(solution)/shard_map/pallas_call | solution.py:32
  103.5 0.0 copy-start.3
  103.5 13.5 %all_to_all.20 = bf16[4,512,128]{2,1,0:T(8,128)(2,1)} all-to-all(bf16[4,512,128]{2,1,0:T(8,128)(2,1)S(1)} %get-tuple-element.21), channel_id=1, replica_groups=mesh['dp'=4,'expert'=128] {'dp'}, dimensions={0} | all-to-all | bytes 1048576 | tf_op jit(solution)/shard_map/all_to_all | solution.py:353
  117.0 21.9 %all-to-all-start.3 = ((bf16[128,16,128]{2,1,0:T(8,128)(2,1)}), bf16[128,16,128]{2,1,0:T(8,128)(2,1)S(1)}, u32[]{:S(2)}, u32[]{:S(2)}) async-start(bf16[128,16,128]{2,1,0:T(8,128)(2,1)} %bitcast.5), calls=%async_computation.3 | async-start | bytes 1048576 | tf_op jit(solution)/shard_map/all_to_all | solution.py:355
  139.0 2.8 %collective-permute-start.6 = (bf16[288,768]{1,0:T(8,128)(2,1)S(1)}, bf16[288,768]{1,0:T(8,128)(2,1)S(1)}, u32[]{:S(2)}, u32[]{:S(2)}) collective-permute-start(bf16[288,768]{1,0:T(8,128)(2,1)S(1)} %get-tuple-element.27.a0_ref), channel_id=1, source_target_pairs={{0,384},{128,0},{256,128},{384,256},{1,385},{129,1},{257,129},{385... | collective-permute-start | bytes 1327112 | tf_op jit(solution)/shard_map/ppermute | solution.py:284
  141.8 3.1 %collective-permute-start.5 = (bf16[288,768]{1,0:T(8,128)(2,1)S(1)}, bf16[288,768]{1,0:T(8,128)(2,1)S(1)}, u32[]{:S(2)}, u32[]{:S(2)}) collective-permute-start(bf16[288,768]{1,0:T(8,128)(2,1)S(1)} %get-tuple-element.27.a0_ref), channel_id=1, source_target_pairs={{0,256},{128,384},{256,0},{384,128},{1,257},{129,385},{257,1},{385... | collective-permute-start | bytes 1327112 | tf_op jit(solution)/shard_map/ppermute | solution.py:284
  144.9 1.9 %collective-permute-start.4 = (bf16[288,768]{1,0:T(8,128)(2,1)S(1)}, bf16[288,768]{1,0:T(8,128)(2,1)S(1)}, u32[]{:S(2)}, u32[]{:S(2)}) collective-permute-start(bf16[288,768]{1,0:T(8,128)(2,1)S(1)} %get-tuple-element.27.a0_ref), channel_id=1, source_target_pairs={{0,128},{128,256},{256,384},{384,0},{1,129},{129,257},{257,385},{3... | collective-permute-start | bytes 1327112 | tf_op jit(solution)/shard_map/ppermute | solution.py:284
  146.8 4.9 %collective-permute-done.6.a3_ref = bf16[288,768]{1,0:T(8,128)(2,1)S(1)} collective-permute-done((bf16[288,768]{1,0:T(8,128)(2,1)S(1)}, bf16[288,768]{1,0:T(8,128)(2,1)S(1)}, u32[]{:S(2)}, u32[]{:S(2)}) %collective-permute-start.6) | collective-permute-done | bytes 442400 | tf_op jit(solution)/shard_map/ppermute | solution.py:284
  151.7 4.1 %collective-permute-done.5.a2_ref = bf16[288,768]{1,0:T(8,128)(2,1)S(1)} collective-permute-done((bf16[288,768]{1,0:T(8,128)(2,1)S(1)}, bf16[288,768]{1,0:T(8,128)(2,1)S(1)}, u32[]{:S(2)}, u32[]{:S(2)}) %collective-permute-start.5) | collective-permute-done | bytes 442400 | tf_op jit(solution)/shard_map/ppermute | solution.py:284
  155.8 11.0 %collective-permute-done.4.a1_ref = bf16[288,768]{1,0:T(8,128)(2,1)S(1)} collective-permute-done((bf16[288,768]{1,0:T(8,128)(2,1)S(1)}, bf16[288,768]{1,0:T(8,128)(2,1)S(1)}, u32[]{:S(2)}, u32[]{:S(2)}) %collective-permute-start.4) | collective-permute-done | bytes 442400 | tf_op jit(solution)/shard_map/ppermute | solution.py:284
  166.7 0.0 copy-done.3
  166.7 0.0 copy-start
  166.7 0.0 copy-start.1
  166.7 0.0 copy-start.2
  166.7 2.3 %shard_map.152 = (bf16[512,768]{1,0:T(8,128)(2,1)}, bf16[512,768]{1,0:T(8,128)(2,1)}, bf16[768,512]{1,0:T(8,128)(2,1)}) custom-call(s32[1]{0:T(128)} %bitcast.2.me_ref, bf16[384,1024]{1,0:T(8,128)(2,1)S(1)} %copy-done.3, bf16[288,768]{1,0:T(8,128)(2,1)S(1)} %get-tuple-element.27.a0_ref, bf16[288,768]{1,0:T(8,128)(2,1)S(1)} %collective-permute-done.4.a1_ref, ...), custom_call_target="tpu_custom_call" | custom-call | flops 905969664 | bytes 4718592 | tf_op jit(solution)/shard_map/pallas_call | solution.py:32
  169.1 3.1 %all-to-all-done.3 = bf16[128,16,128]{2,1,0:T(8,128)(2,1)S(1)} async-done(((bf16[128,16,128]{2,1,0:T(8,128)(2,1)}), bf16[128,16,128]{2,1,0:T(8,128)(2,1)S(1)}, u32[]{:S(2)}, u32[]{:S(2)}) %all-to-all-start.3) | async-done | bytes 524320 | tf_op jit(solution)/shard_map/all_to_all | solution.py:355
  172.2 0.0 copy-done
  172.2 0.0 copy-done.1
  172.2 0.0 copy-done.2
  172.2 1.2 shard_map.151
Async XLA Ops:
  3.9 74.8 %all-to-all-start = ((bf16[128,24,128]{2,1,0:T(8,128)(2,1)}), bf16[128,24,128]{2,1,0:T(8,128)(2,1)}, u32[]{:S(2)}, u32[]{:S(2)}) async-start(bf16[128,24,128]{2,1,0:T(8,128)(2,1)} %bitcast.13), calls=%async_computation | async-start | bytes 1572864 | tf_op jit(solution)/shard_map/all_to_all | solution.py:305
  27.6 48.3 %copy-start.6 = (f32[6,4]{0,1:T(4,128)S(1)}, f32[6,4]{0,1:T(4,128)}, u32[]{:S(2)}) copy-start(f32[6,4]{0,1:T(4,128)} %param.20) | copy-start | bytes 292
  27.6 38.7 %collective-permute-start.2 = (bf16[1024,768]{1,0:T(8,128)(2,1)}, bf16[1024,768]{1,0:T(8,128)(2,1)S(1)}, u32[]{:S(2)}, u32[]{:S(2)}) collective-permute-start(bf16[1024,768]{1,0:T(8,128)(2,1)} %shard_map.149.own_hbm), channel_id=1, source_target_pairs={{0,128},{128,256},{256,384},{384,0},{1,129},{129,257},{257,385},{3... | collective-permute-start | bytes 4718600 | tf_op jit(solution)/shard_map/ppermute | solution.py:284
  30.9 38.3 %collective-permute-start = (bf16[1024,768]{1,0:T(8,128)(2,1)}, bf16[1024,768]{1,0:T(8,128)(2,1)S(1)}, u32[]{:S(2)}, u32[]{:S(2)}) collective-permute-start(bf16[1024,768]{1,0:T(8,128)(2,1)} %shard_map.149.own_hbm), channel_id=1, source_target_pairs={{0,384},{128,0},{256,128},{384,256},{1,385},{129,1},{257,129},{385... | collective-permute-start | bytes 4718600 | tf_op jit(solution)/shard_map/ppermute | solution.py:284
  66.3 5.0 %copy-start.4 = (bf16[1024,768]{1,0:T(8,128)(2,1)}, bf16[1024,768]{1,0:T(8,128)(2,1)S(1)}, u32[]{:S(2)}) copy-start(bf16[1024,768]{1,0:T(8,128)(2,1)S(1)} %collective-permute-done.2.prev_hbm) | copy-start | bytes 4718596
  67.3 20.8 %collective-permute-start.3 = (bf16[512,768]{1,0:T(8,128)(2,1)}, bf16[512,768]{1,0:T(8,128)(2,1)S(1)}, u32[]{:S(2)}, u32[]{:S(2)}) collective-permute-start(bf16[512,768]{1,0:T(8,128)(2,1)} %slice.9), channel_id=1, source_target_pairs={{0,128},{128,256},{256,384},{384,0},{1,129},{129,257},{257,385},{3... | collective-permute-start | bytes 2359304 | tf_op jit(solution)/shard_map/ppermute | solution.py:284
  69.2 1.2 copy-start.5
  71.3 19.8 %collective-permute-start.1 = (bf16[512,768]{1,0:T(8,128)(2,1)}, bf16[512,768]{1,0:T(8,128)(2,1)S(1)}, u32[]{:S(2)}, u32[]{:S(2)}) collective-permute-start(bf16[512,768]{1,0:T(8,128)(2,1)} %slice.8), channel_id=1, source_target_pairs={{0,384},{128,0},{256,128},{384,256},{1,385},{129,1},{257,129},{385... | collective-permute-start | bytes 2359304 | tf_op jit(solution)/shard_map/ppermute | solution.py:284
  81.8 16.5 %all-to-all-start.1 = ((bf16[4,96,1280]{2,1,0:T(8,128)(2,1)}), bf16[4,96,1280]{2,1,0:T(8,128)(2,1)S(1)}, u32[]{:S(2)}, u32[]{:S(2)}) async-start(bf16[4,96,1280]{2,1,0:T(8,128)(2,1)} %get-tuple-element.20), calls=%async_computation.1 | async-start | bytes 1966080 | tf_op jit(solution)/shard_map/all_to_all | solution.py:335
  103.5 63.2 %copy-start.3 = (bf16[384,1024]{1,0:T(8,128)(2,1)S(1)}, bf16[384,1024]{1,0:T(8,128)(2,1)}, u32[]{:S(2)}) copy-start(bf16[384,1024]{1,0:T(8,128)(2,1)} %get-tuple-element.26.rows_ref) | copy-start | bytes 2359300
  117.0 55.2 %all-to-all-start.3 = ((bf16[128,16,128]{2,1,0:T(8,128)(2,1)}), bf16[128,16,128]{2,1,0:T(8,128)(2,1)S(1)}, u32[]{:S(2)}, u32[]{:S(2)}) async-start(bf16[128,16,128]{2,1,0:T(8,128)(2,1)} %bitcast.5), calls=%async_computation.3 | async-start | bytes 1048576 | tf_op jit(solution)/shard_map/all_to_all | solution.py:355
  139.0 12.7 %collective-permute-start.6 = (bf16[288,768]{1,0:T(8,128)(2,1)S(1)}, bf16[288,768]{1,0:T(8,128)(2,1)S(1)}, u32[]{:S(2)}, u32[]{:S(2)}) collective-permute-start(bf16[288,768]{1,0:T(8,128)(2,1)S(1)} %get-tuple-element.27.a0_ref), channel_id=1, source_target_pairs={{0,384},{128,0},{256,128},{384,256},{1,385},{129,1},{257,129},{385... | collective-permute-start | bytes 1327112 | tf_op jit(solution)/shard_map/ppermute | solution.py:284
  141.8 14.0 %collective-permute-start.5 = (bf16[288,768]{1,0:T(8,128)(2,1)S(1)}, bf16[288,768]{1,0:T(8,128)(2,1)S(1)}, u32[]{:S(2)}, u32[]{:S(2)}) collective-permute-start(bf16[288,768]{1,0:T(8,128)(2,1)S(1)} %get-tuple-element.27.a0_ref), channel_id=1, source_target_pairs={{0,256},{128,384},{256,0},{384,128},{1,257},{129,385},{257,1},{385... | collective-permute-start | bytes 1327112 | tf_op jit(solution)/shard_map/ppermute | solution.py:284
  144.9 21.9 %collective-permute-start.4 = (bf16[288,768]{1,0:T(8,128)(2,1)S(1)}, bf16[288,768]{1,0:T(8,128)(2,1)S(1)}, u32[]{:S(2)}, u32[]{:S(2)}) collective-permute-start(bf16[288,768]{1,0:T(8,128)(2,1)S(1)} %get-tuple-element.27.a0_ref), channel_id=1, source_target_pairs={{0,128},{128,256},{256,384},{384,0},{1,129},{129,257},{257,385},{3... | collective-permute-start | bytes 1327112 | tf_op jit(solution)/shard_map/ppermute | solution.py:284
  166.7 5.4 %copy-start = (bf16[384,128]{1,0:T(8,128)(2,1)S(1)}, bf16[384,128]{1,0:T(8,128)(2,1)}, u32[]{:S(2)}) copy-start(bf16[384,128]{1,0:T(8,128)(2,1)} %get-tuple-element.18.slots_ref) | copy-start | bytes 294916
  166.7 5.4 %copy-start.1 = (s32[128,2]{0,1:T(2,128)S(1)}, s32[128,2]{0,1:T(2,128)}, u32[]{:S(2)}) copy-start(s32[128,2]{0,1:T(2,128)} %param.12) | copy-start | bytes 3076
  166.7 5.4 %copy-start.2 = (f32[128,2]{0,1:T(2,128)S(1)}, f32[128,2]{0,1:T(2,128)}, u32[]{:S(2)}) copy-start(f32[128,2]{0,1:T(2,128)} %param.13) | copy-start | bytes 3076

commit v5 on v4

--- a/solution.py
+++ b/solution.py
@@ -81,9 +81,23 @@
             ).astype(BF)
 
 
-def dequant_pair_kernel(gs_ref, us_ref, gc_ref, uc_ref, out_ref):
-    dequant(gs_ref, gc_ref, out_ref, 0)
-    dequant(us_ref, uc_ref, out_ref, gc_ref.shape[0])
+def dequant_pair_kernel(gs_ref, us_ref, gc_hbm, uc_hbm, out_hbm, code_ref, out_ref, sems):
+    half = code_ref.shape[1]
+    load = [
+        pltpu.make_async_copy(source, code_ref.at[n], sems.at[n])
+        for n, source in enumerate((gc_hbm, uc_hbm))
+    ]
+    for copy in load:
+        copy.start()
+    save = []
+    for n, scale_ref in enumerate((gs_ref, us_ref)):
+        load[n].wait()
+        dequant(scale_ref, code_ref.at[n], out_ref, n * half)
+        lines = slice(n * half, (n + 1) * half)
+        save.append(pltpu.make_async_copy(out_ref.at[lines], out_hbm.at[lines], sems.at[2 + n]))
+        save[n].start()
+    for copy in save:
+        copy.wait()
 
 
 def dequant_one_kernel(ds_ref, dc_ref, out_ref):
@@ -105,35 +119,42 @@
         copy.start()
     load[0].wait()
     mix_ref[...] = got_ref[...].astype(F32)
-    for kind in range(2):
+
+    def unpack(kind, targets):
         for p in range(CAP):
             for h in range(wide):
                 at = (kind * CAP + p) * wide + h
-                lane = kind * quarter + h * LANES
                 value = mix_ref[pl.ds(at, groups, stride=chunks), :].astype(BF)
                 for j in range(parts):
-                    line = j * span + p * near
-                    piece = value[j * near : (j + 1) * near]
-                    rows_ref[line : line + near, lane : lane + LANES] = piece
-                    if kind == 0:
-                        out_ref[j, p * near : (p + 1) * near, lane : lane + LANES] = piece
-    save = [pltpu.make_async_copy(rows_ref, rows_hbm, sems.at[2])]
-    save[0].start()
+                    for target, lines, lane in targets(j, p * near):
+                        target[lines, lane + h * LANES : lane + (h + 1) * LANES] = value[
+                            j * near : (j + 1) * near
+                        ]
+
+    def whole(j, line, lane):
+        return (rows_ref, slice(j * span + line, j * span + line + near), lane)
+
+    unpack(1, lambda j, line: [whole(j, line, quarter)])
     load[1].wait()
     back = lax.dot_general(
         rows_ref[:, quarter:], wd_ref[...], LAST, preferred_element_type=F32
     ).astype(BF)
+    unpack(
+        0,
+        lambda j, line: [whole(j, line, 0), (out_ref.at[j], slice(line, line + near), 0)],
+    )
+    save = [pltpu.make_async_copy(rows_ref, rows_hbm, sems.at[2])]
     for j in range(parts):
         out_ref[j, :, quarter:] = back[j * span : (j + 1) * span]
-        copy = pltpu.make_async_copy(out_ref.at[j], out_hbm.at[j], sems.at[3 + j])
+        save.append(pltpu.make_async_copy(out_ref.at[j], out_hbm.at[j], sems.at[3 + j]))
+    for copy in save:
         copy.start()
-        save.append(copy)
     for copy in save:
         copy.wait()
 
 
 def act_kernel(
-    me_ref, part_ref, own_hbm, next_hbm, far_gate_hbm, far_up_hbm, prev_hbm, out_ref, act_ref, w_ref, mix_ref, sems
+    me_ref, part_ref, own_hbm, next_hbm, far_low_hbm, far_high_hbm, prev_hbm, out_ref, act_ref, w_ref, mix_ref, sems
 ):
     parts, span, _ = part_ref.shape
     near = span // CAP
@@ -148,8 +169,8 @@
                 (own_hbm, w_ref.at[0]),
                 (next_hbm, w_ref.at[1]),
                 (prev_hbm, w_ref.at[3]),
-                (far_gate_hbm, w_ref.at[2, :quarter]),
-                (far_up_hbm, w_ref.at[2, quarter:]),
+                (far_low_hbm, w_ref.at[2, :quarter]),
+                (far_high_hbm, w_ref.at[2, quarter:]),
             )
         )
     ]
@@ -286,10 +307,16 @@
     w_own = call(
         dequant_pair_kernel,
         shape((2 * quarter, hidden_size), BF),
-        [SMEM] * 2 + [VMEM] * 2,
+        [SMEM] * 2 + [ANY] * 2,
         (gate_scales, up_scales, gate_codes, up_codes),
         flops=2 * quarter * hidden_size,
         nbytes=8 * quarter * hidden_size,
+        scratch=[
+            pltpu.VMEM((2, quarter, hidden_size), BF),
+            pltpu.VMEM((2 * quarter, hidden_size), BF),
+            pltpu.SemaphoreType.DMA((4,)),
+        ],
+        place=ANY,
     )
     w_prev = turn(w_own, 1)
     w_next = turn(w_own, -1)
@@ -298,6 +325,7 @@
         (shape((experts * out_chunks, LANES), BF), shape((slots, count), BF)),
         [SMEM, VMEM, VMEM, VMEM, VMEM],
         (live_tokens, routes_t, weights_t, tokens, grad_out),
+        grant=SMALL,
         flops=2 * slots * count * quarter * 4,
         nbytes=2 * slots * 2 * quarter,
         scratch=[pltpu.VMEM((experts * out_chunks, LANES), F32)],
@@ -305,8 +333,8 @@
     got = lax.all_to_all(
         send.reshape(experts, out_chunks, LANES), "expert", split_axis=0, concat_axis=0, tiled=True
     )
-    far_gate = turn(w_next[:quarter], -1)
-    far_up = turn(w_prev[quarter:], 1)
+    far_low = turn(w_next[:quarter], -1)
+    far_high = turn(w_prev[quarter:], 1)
     w_down = call(
         dequant_one_kernel,
         shape(down_codes.shape, BF),
@@ -340,7 +368,7 @@
             shape((3 * span, hidden_size), BF),
         ),
         [SMEM, VMEM] + [ANY] * 5,
-        (me.reshape(1), part, w_own, w_next, far_gate, far_up, w_prev),
+        (me.reshape(1), part, w_own, w_next, far_low, far_high, w_prev),
         grant=MIDDLE,
         flops=8 * slots * quarter * hidden_size,
         nbytes=16 * quarter * hidden_size,

time: 174 us -> 177 us (1.017)
  local copies, waits for them, and re-layouts: 3.81 us -> 8.03 us
    unnamed x15 -> x25, local copies, waits for them, and re-layouts: 1.86 us -> 6.05 us
where the time goes in v5:
time: 177 us; the launch traced here: 176 us
  starting transfers between devices  67.1 us (38%)
  waiting for transfers between devices  66.4 us (38%)
  Pallas kernels  19.1 us (11%)
  blocking collectives  13.8 us (8%)
  local copies, waits for them, and re-layouts  8.03 us (5%)
    ppermute x7, waiting for transfers between devices, turn(): lax.ppermute(value, 'dp', [(i, (i + shift) % parts) for i in range(parts)])  57.7 us
    all_to_all x1, starting transfers between devices, layer(): lax.all_to_all(ret.reshape(experts, back_chunks, LANES), 'expert', split_...  22 us
    ppermute x7, starting transfers between devices, turn(): lax.ppermute(value, 'dp', [(i, (i + shift) % parts) for i in range(parts)])  20.8 us
    all_to_all x1, starting transfers between devices, layer(): lax.all_to_all(send.reshape(experts, out_chunks, LANES), 'expert', split_...  20.8 us
    pallas_call x7, Pallas kernels, call(): pl.pallas_call(kernel, out_shape=outs, in_specs=in_specs, out_specs=jax.t...  19.1 us
    all_to_all x1, blocking collectives, layer(): ret = lax.all_to_all(ret, 'dp', split_axis=0, concat_axis=0, tiled=True)  13.8 us
    all_to_all x1, waiting for transfers between devices, layer(): part = lax.all_to_all(part, 'dp', split_axis=0, concat_axis=0, tiled=True)  6.83 us
    unnamed x25, local copies, waits for them, and re-layouts  6.05 us
  transfers between devices with their start and end apart: 10, of which 8 were waited for; matrix products, arithmetic and copies ran while one was open for 2% of the time, Pallas kernels for 6%

profile of v5, /device:TPU:1, one launch (start us, length us, event | category | flops | bytes accessed | tf_op | source)
XLA Modules:
  0.0 175.8 jit_solution(9713420591391709650)
XLA Ops:
  1.3 0.0 copy-start
  1.3 0.7 copy-done
  2.0 0.7 copy-done.2
  2.6 0.9 copy-done.7
  3.5 0.9 copy-done.8
  4.4 1.7 shard_map.146
  6.1 20.8 %all-to-all-start = ((bf16[128,24,128]{2,1,0:T(8,128)(2,1)}), bf16[128,24,128]{2,1,0:T(8,128)(2,1)}, u32[]{:S(2)}, u32[]{:S(2)}) async-start(bf16[128,24,128]{2,1,0:T(8,128)(2,1)} %bitcast.3), calls=%async_computation | async-start | bytes 1572864 | tf_op jit(solution)/shard_map/all_to_all | solution.py:333
  26.9 3.2 %shard_map.149.own_hbm = bf16[1024,768]{1,0:T(8,128)(2,1)} custom-call(f32[4,6]{1,0:T(4,128)} %gs_ref.1, f32[4,6]{1,0:T(4,128)} %us_ref.1, bf16[512,768]{1,0:T(8,128)(2,1)} %gc_hbm.1, bf16[512,768]{1,0:T(8,128)(2,1)} %uc_hbm.1), custom_call_target="tpu_custom_call" | custom-call | flops 786432 | bytes 3145728 | tf_op jit(solution)/shard_map/pallas_call | solution.py:32
  30.1 0.0 copy-start.11
  30.1 3.2 %collective-permute-start.2 = (bf16[1024,768]{1,0:T(8,128)(2,1)}, bf16[1024,768]{1,0:T(8,128)(2,1)S(1)}, u32[]{:S(2)}, u32[]{:S(2)}) collective-permute-start(bf16[1024,768]{1,0:T(8,128)(2,1)} %shard_map.149.own_hbm), channel_id=1, source_target_pairs={{0,128},{128,256},{256,384},{384,0},{1,129},{129,257},{257,385},{3... | collective-permute-start | bytes 4718600 | tf_op jit(solution)/shard_map/ppermute | solution.py:305
  33.4 3.4 %collective-permute-start = (bf16[1024,768]{1,0:T(8,128)(2,1)}, bf16[1024,768]{1,0:T(8,128)(2,1)S(1)}, u32[]{:S(2)}, u32[]{:S(2)}) collective-permute-start(bf16[1024,768]{1,0:T(8,128)(2,1)} %shard_map.149.own_hbm), channel_id=1, source_target_pairs={{0,384},{128,0},{256,128},{384,256},{1,385},{129,1},{257,129},{385... | collective-permute-start | bytes 4718600 | tf_op jit(solution)/shard_map/ppermute | solution.py:305
  36.7 32.0 %collective-permute-done.2.prev_hbm = bf16[1024,768]{1,0:T(8,128)(2,1)S(1)} collective-permute-done((bf16[1024,768]{1,0:T(8,128)(2,1)}, bf16[1024,768]{1,0:T(8,128)(2,1)S(1)}, u32[]{:S(2)}, u32[]{:S(2)}) %collective-permute-start.2) | collective-permute-done | bytes 1572896 | tf_op jit(solution)/shard_map/ppermute | solution.py:305
  68.7 1.1 slice.9
  69.8 1.9 %collective-permute-start.3 = (bf16[512,768]{1,0:T(8,128)(2,1)}, bf16[512,768]{1,0:T(8,128)(2,1)S(1)}, u32[]{:S(2)}, u32[]{:S(2)}) collective-permute-start(bf16[512,768]{1,0:T(8,128)(2,1)} %slice.9), channel_id=1, source_target_pairs={{0,128},{128,256},{256,384},{384,0},{1,129},{129,257},{257,385},{3... | collective-permute-start | bytes 2359304 | tf_op jit(solution)/shard_map/ppermute | solution.py:305
  71.7 0.0 collective-permute-done.next_hbm
  71.7 0.0 copy-start.10
  71.7 1.2 copy-done.10
  72.9 0.9 slice.8
  73.8 0.0 copy-done.9
  73.8 4.6 %collective-permute-start.1 = (bf16[512,768]{1,0:T(8,128)(2,1)}, bf16[512,768]{1,0:T(8,128)(2,1)S(1)}, u32[]{:S(2)}, u32[]{:S(2)}) collective-permute-start(bf16[512,768]{1,0:T(8,128)(2,1)} %slice.8), channel_id=1, source_target_pairs={{0,384},{128,0},{256,128},{384,256},{1,385},{129,1},{257,129},{385... | collective-permute-start | bytes 2359304 | tf_op jit(solution)/shard_map/ppermute | solution.py:305
  78.4 0.0 copy-done.11
  78.4 0.7 copy.16.ds_ref
  79.0 2.2 %shard_map.147.wd_hbm = bf16[768,512]{1,0:T(8,128)(2,1)} custom-call(f32[6,4]{1,0:T(8,128)} %copy.16.ds_ref, bf16[768,512]{1,0:T(8,128)(2,1)} %dc_ref.1), custom_call_target="tpu_custom_call" | custom-call | flops 393216 | bytes 1572864 | tf_op jit(solution)/shard_map/pallas_call | solution.py:32
  81.2 0.0 all-to-all-done
  81.2 3.3 %shard_map.148 = (bf16[4,96,1280]{2,1,0:T(8,128)(2,1)}, bf16[384,1024]{1,0:T(8,128)(2,1)}) custom-call(bf16[3072,128]{1,0:T(8,128)(2,1)} %bitcast.4.got_hbm, bf16[768,512]{1,0:T(8,128)(2,1)} %shard_map.147.wd_hbm), custom_call_target="tpu_custom_call" | custom-call | flops 301989888 | bytes 2359296 | tf_op jit(solution)/shard_map/pallas_call | solution.py:32
  84.5 3.5 %all-to-all-start.1 = ((bf16[4,96,1280]{2,1,0:T(8,128)(2,1)}), bf16[4,96,1280]{2,1,0:T(8,128)(2,1)S(1)}, u32[]{:S(2)}, u32[]{:S(2)}) async-start(bf16[4,96,1280]{2,1,0:T(8,128)(2,1)} %get-tuple-element.20), calls=%async_computation.1 | async-start | bytes 1966080 | tf_op jit(solution)/shard_map/all_to_all | solution.py:363
  88.0 2.5 %collective-permute-done.3.far_high_hbm = bf16[512,768]{1,0:T(8,128)(2,1)S(1)} collective-permute-done((bf16[512,768]{1,0:T(8,128)(2,1)}, bf16[512,768]{1,0:T(8,128)(2,1)S(1)}, u32[]{:S(2)}, u32[]{:S(2)}) %collective-permute-start.3) | collective-permute-done | bytes 786464 | tf_op jit(solution)/shard_map/ppermute | solution.py:305
  90.5 3.1 %collective-permute-done.1.far_low_hbm = bf16[512,768]{1,0:T(8,128)(2,1)S(1)} collective-permute-done((bf16[512,768]{1,0:T(8,128)(2,1)}, bf16[512,768]{1,0:T(8,128)(2,1)S(1)}, u32[]{:S(2)}, u32[]{:S(2)}) %collective-permute-start.1) | collective-permute-done | bytes 786464 | tf_op jit(solution)/shard_map/ppermute | solution.py:305
  93.6 6.8 %all-to-all-done.1.part_ref = bf16[4,96,1280]{2,1,0:T(8,128)(2,1)S(1)} async-done(((bf16[4,96,1280]{2,1,0:T(8,128)(2,1)}), bf16[4,96,1280]{2,1,0:T(8,128)(2,1)S(1)}, u32[]{:S(2)}, u32[]{:S(2)}) %all-to-all-start.1) | async-done | bytes 983072 | tf_op jit(solution)/shard_map/all_to_all | solution.py:363
  100.5 5.2 %shard_map.150 = (bf16[4,512,128]{2,1,0:T(8,128)(2,1)S(1)}, bf16[288,768]{1,0:T(8,128)(2,1)S(1)}) custom-call(s32[1]{0:T(128)} %bitcast.2.me_ref, bf16[4,96,1280]{2,1,0:T(8,128)(2,1)S(1)} %all-to-all-done.1.part_ref, bf16[1024,768]{1,0:T(8,128)(2,1)} %shard_map.149.own_hbm, bf16[1024,768]{1,0:T(8,128)(2,1)} %copy-done.10, ...), custom_call_target="tpu_custom_call" | custom-call | flops 1207959552 | bytes 6291456 | tf_op jit(solution)/shard_map/pallas_call | solution.py:32
  105.7 0.0 copy-start.5
  105.7 0.0 copy-start.4
  105.7 13.8 %all_to_all.20 = bf16[4,512,128]{2,1,0:T(8,128)(2,1)} all-to-all(bf16[4,512,128]{2,1,0:T(8,128)(2,1)S(1)} %get-tuple-element.21), channel_id=1, replica_groups=mesh['dp'=4,'expert'=128] {'dp'}, dimensions={0} | all-to-all | bytes 1048576 | tf_op jit(solution)/shard_map/all_to_all | solution.py:381
  119.5 0.0 copy-done.5
  119.5 22.0 %all-to-all-start.3 = ((bf16[128,16,128]{2,1,0:T(8,128)(2,1)}), bf16[128,16,128]{2,1,0:T(8,128)(2,1)S(1)}, u32[]{:S(2)}, u32[]{:S(2)}) async-start(bf16[128,16,128]{2,1,0:T(8,128)(2,1)} %bitcast.5), calls=%async_computation.3 | async-start | bytes 1048576 | tf_op jit(solution)/shard_map/all_to_all | solution.py:383
  141.5 2.8 %collective-permute-start.6 = (bf16[288,768]{1,0:T(8,128)(2,1)}, bf16[288,768]{1,0:T(8,128)(2,1)S(1)}, u32[]{:S(2)}, u32[]{:S(2)}) collective-permute-start(bf16[288,768]{1,0:T(8,128)(2,1)} %copy-done.5), channel_id=1, source_target_pairs={{0,384},{128,0},{256,128},{384,256},{1,385},{129,1},{257,129},{385... | collective-permute-start | bytes 1327112 | tf_op jit(solution)/shard_map/ppermute | solution.py:305
  144.3 3.1 %collective-permute-start.5 = (bf16[288,768]{1,0:T(8,128)(2,1)}, bf16[288,768]{1,0:T(8,128)(2,1)S(1)}, u32[]{:S(2)}, u32[]{:S(2)}) collective-permute-start(bf16[288,768]{1,0:T(8,128)(2,1)} %copy-done.5), channel_id=1, source_target_pairs={{0,256},{128,384},{256,0},{384,128},{1,257},{129,385},{257,1},{385... | collective-permute-start | bytes 1327112 | tf_op jit(solution)/shard_map/ppermute | solution.py:305
  147.4 1.9 %collective-permute-start.4 = (bf16[288,768]{1,0:T(8,128)(2,1)}, bf16[288,768]{1,0:T(8,128)(2,1)S(1)}, u32[]{:S(2)}, u32[]{:S(2)}) collective-permute-start(bf16[288,768]{1,0:T(8,128)(2,1)} %copy-done.5), channel_id=1, source_target_pairs={{0,128},{128,256},{256,384},{384,0},{1,129},{129,257},{257,385},{3... | collective-permute-start | bytes 1327112 | tf_op jit(solution)/shard_map/ppermute | solution.py:305
  149.3 5.1 %collective-permute-done.6.a3_ref = bf16[288,768]{1,0:T(8,128)(2,1)S(1)} collective-permute-done((bf16[288,768]{1,0:T(8,128)(2,1)}, bf16[288,768]{1,0:T(8,128)(2,1)S(1)}, u32[]{:S(2)}, u32[]{:S(2)}) %collective-permute-start.6) | collective-permute-done | bytes 442400 | tf_op jit(solution)/shard_map/ppermute | solution.py:305
  154.4 4.1 %collective-permute-done.5.a2_ref = bf16[288,768]{1,0:T(8,128)(2,1)S(1)} collective-permute-done((bf16[288,768]{1,0:T(8,128)(2,1)}, bf16[288,768]{1,0:T(8,128)(2,1)S(1)}, u32[]{:S(2)}, u32[]{:S(2)}) %collective-permute-start.5) | collective-permute-done | bytes 442400 | tf_op jit(solution)/shard_map/ppermute | solution.py:305
  158.5 11.0 %collective-permute-done.4.a1_ref = bf16[288,768]{1,0:T(8,128)(2,1)S(1)} collective-permute-done((bf16[288,768]{1,0:T(8,128)(2,1)}, bf16[288,768]{1,0:T(8,128)(2,1)S(1)}, u32[]{:S(2)}, u32[]{:S(2)}) %collective-permute-start.4) | collective-permute-done | bytes 442400 | tf_op jit(solution)/shard_map/ppermute | solution.py:305
  169.4 0.0 copy-done.4
  169.5 1.0 copy-done.6
  170.5 2.3 %shard_map.152 = (bf16[512,768]{1,0:T(8,128)(2,1)}, bf16[512,768]{1,0:T(8,128)(2,1)}, bf16[768,512]{1,0:T(8,128)(2,1)}) custom-call(s32[1]{0:T(128)} %bitcast.2.me_ref, bf16[384,1024]{1,0:T(8,128)(2,1)S(1)} %copy-done.4, bf16[288,768]{1,0:T(8,128)(2,1)S(1)} %copy-done.6, bf16[288,768]{1,0:T(8,128)(2,1)S(1)} %collective-permute-done.4.a1_ref, ...), custom_call_target="tpu_custom_call" | custom-call | flops 905969664 | bytes 4718592 | tf_op jit(solution)/shard_map/pallas_call | solution.py:32
  172.8 1.9 %all-to-all-done.3 = bf16[128,16,128]{2,1,0:T(8,128)(2,1)S(1)} async-done(((bf16[128,16,128]{2,1,0:T(8,128)(2,1)}), bf16[128,16,128]{2,1,0:T(8,128)(2,1)S(1)}, u32[]{:S(2)}, u32[]{:S(2)}) %all-to-all-start.3) | async-done | bytes 524320 | tf_op jit(solution)/shard_map/all_to_all | solution.py:383
  174.7 0.0 copy-done.1
  174.7 0.0 copy-done.3
  174.7 1.2 shard_map.151
  (7 shorter events, 0.0 us)
Async XLA Ops:
  1.3 0.7 copy-start
  2.0 0.7 copy-start.2
  2.6 0.9 copy-start.7
  3.5 0.9 copy-start.8
  6.1 75.1 %all-to-all-start = ((bf16[128,24,128]{2,1,0:T(8,128)(2,1)}), bf16[128,24,128]{2,1,0:T(8,128)(2,1)}, u32[]{:S(2)}, u32[]{:S(2)}) async-start(bf16[128,24,128]{2,1,0:T(8,128)(2,1)} %bitcast.3), calls=%async_computation | async-start | bytes 1572864 | tf_op jit(solution)/shard_map/all_to_all | solution.py:333
  30.1 48.2 %copy-start.11 = (f32[6,4]{0,1:T(4,128)S(1)}, f32[6,4]{0,1:T(4,128)}, u32[]{:S(2)}) copy-start(f32[6,4]{0,1:T(4,128)} %param.20) | copy-start | bytes 292
  30.1 38.6 %collective-permute-start.2 = (bf16[1024,768]{1,0:T(8,128)(2,1)}, bf16[1024,768]{1,0:T(8,128)(2,1)S(1)}, u32[]{:S(2)}, u32[]{:S(2)}) collective-permute-start(bf16[1024,768]{1,0:T(8,128)(2,1)} %shard_map.149.own_hbm), channel_id=1, source_target_pairs={{0,128},{128,256},{256,384},{384,0},{1,129},{129,257},{257,385},{3... | collective-permute-start | bytes 4718600 | tf_op jit(solution)/shard_map/ppermute | solution.py:305
  33.4 38.3 %collective-permute-start = (bf16[1024,768]{1,0:T(8,128)(2,1)}, bf16[1024,768]{1,0:T(8,128)(2,1)S(1)}, u32[]{:S(2)}, u32[]{:S(2)}) collective-permute-start(bf16[1024,768]{1,0:T(8,128)(2,1)} %shard_map.149.own_hbm), channel_id=1, source_target_pairs={{0,384},{128,0},{256,128},{384,256},{1,385},{129,1},{257,129},{385... | collective-permute-start | bytes 4718600 | tf_op jit(solution)/shard_map/ppermute | solution.py:305
  68.7 5.1 %copy-start.9 = (bf16[1024,768]{1,0:T(8,128)(2,1)}, bf16[1024,768]{1,0:T(8,128)(2,1)S(1)}, u32[]{:S(2)}) copy-start(bf16[1024,768]{1,0:T(8,128)(2,1)S(1)} %collective-permute-done.2.prev_hbm) | copy-start | bytes 4718596
  69.8 20.8 %collective-permute-start.3 = (bf16[512,768]{1,0:T(8,128)(2,1)}, bf16[512,768]{1,0:T(8,128)(2,1)S(1)}, u32[]{:S(2)}, u32[]{:S(2)}) collective-permute-start(bf16[512,768]{1,0:T(8,128)(2,1)} %slice.9), channel_id=1, source_target_pairs={{0,128},{128,256},{256,384},{384,0},{1,129},{129,257},{257,385},{3... | collective-permute-start | bytes 2359304 | tf_op jit(solution)/shard_map/ppermute | solution.py:305
  71.7 1.2 copy-start.10
  73.8 19.8 %collective-permute-start.1 = (bf16[512,768]{1,0:T(8,128)(2,1)}, bf16[512,768]{1,0:T(8,128)(2,1)S(1)}, u32[]{:S(2)}, u32[]{:S(2)}) collective-permute-start(bf16[512,768]{1,0:T(8,128)(2,1)} %slice.8), channel_id=1, source_target_pairs={{0,384},{128,0},{256,128},{384,256},{1,385},{129,1},{257,129},{385... | collective-permute-start | bytes 2359304 | tf_op jit(solution)/shard_map/ppermute | solution.py:305
  84.5 16.0 %all-to-all-start.1 = ((bf16[4,96,1280]{2,1,0:T(8,128)(2,1)}), bf16[4,96,1280]{2,1,0:T(8,128)(2,1)S(1)}, u32[]{:S(2)}, u32[]{:S(2)}) async-start(bf16[4,96,1280]{2,1,0:T(8,128)(2,1)} %get-tuple-element.20), calls=%async_computation.1 | async-start | bytes 1966080 | tf_op jit(solution)/shard_map/all_to_all | solution.py:363
  105.7 13.8 %copy-start.5 = (bf16[288,768]{1,0:T(8,128)(2,1)}, bf16[288,768]{1,0:T(8,128)(2,1)S(1)}, u32[]{:S(2)}) copy-start(bf16[288,768]{1,0:T(8,128)(2,1)S(1)} %get-tuple-element.27.a0_ref) | copy-start | bytes 1327108
  105.7 63.7 %copy-start.4 = (bf16[384,1024]{1,0:T(8,128)(2,1)S(1)}, bf16[384,1024]{1,0:T(8,128)(2,1)}, u32[]{:S(2)}) copy-start(bf16[384,1024]{1,0:T(8,128)(2,1)} %get-tuple-element.26.rows_ref) | copy-start | bytes 2359300
  119.5 55.2 %all-to-all-start.3 = ((bf16[128,16,128]{2,1,0:T(8,128)(2,1)}), bf16[128,16,128]{2,1,0:T(8,128)(2,1)S(1)}, u32[]{:S(2)}, u32[]{:S(2)}) async-start(bf16[128,16,128]{2,1,0:T(8,128)(2,1)} %bitcast.5), calls=%async_computation.3 | async-start | bytes 1048576 | tf_op jit(solution)/shard_map/all_to_all | solution.py:383
  141.5 12.9 %collective-permute-start.6 = (bf16[288,768]{1,0:T(8,128)(2,1)}, bf16[288,768]{1,0:T(8,128)(2,1)S(1)}, u32[]{:S(2)}, u32[]{:S(2)}) collective-permute-start(bf16[288,768]{1,0:T(8,128)(2,1)} %copy-done.5), channel_id=1, source_target_pairs={{0,384},{128,0},{256,128},{384,256},{1,385},{129,1},{257,129},{385... | collective-permute-start | bytes 1327112 | tf_op jit(solution)/shard_map/ppermute | solution.py:305
  144.3 14.2 %collective-permute-start.5 = (bf16[288,768]{1,0:T(8,128)(2,1)}, bf16[288,768]{1,0:T(8,128)(2,1)S(1)}, u32[]{:S(2)}, u32[]{:S(2)}) collective-permute-start(bf16[288,768]{1,0:T(8,128)(2,1)} %copy-done.5), channel_id=1, source_target_pairs={{0,256},{128,384},{256,0},{384,128},{1,257},{129,385},{257,1},{385... | collective-permute-start | bytes 1327112 | tf_op jit(solution)/shard_map/ppermute | solution.py:305
  147.4 22.1 %collective-permute-start.4 = (bf16[288,768]{1,0:T(8,128)(2,1)}, bf16[288,768]{1,0:T(8,128)(2,1)S(1)}, u32[]{:S(2)}, u32[]{:S(2)}) collective-permute-start(bf16[288,768]{1,0:T(8,128)(2,1)} %copy-done.5), channel_id=1, source_target_pairs={{0,128},{128,256},{256,384},{384,0},{1,129},{129,257},{257,385},{3... | collective-permute-start | bytes 1327112 | tf_op jit(solution)/shard_map/ppermute | solution.py:305
  169.4 1.0 copy-start.6
  170.5 4.2 %copy-start.1 = (s32[128,2]{0,1:T(2,128)S(1)}, s32[128,2]{0,1:T(2,128)}, u32[]{:S(2)}) copy-start(s32[128,2]{0,1:T(2,128)} %param.12) | copy-start | bytes 3076
  170.5 4.2 %copy-start.3 = (f32[128,2]{0,1:T(2,128)S(1)}, f32[128,2]{0,1:T(2,128)}, u32[]{:S(2)}) copy-start(f32[128,2]{0,1:T(2,128)} %param.13) | copy-start | bytes 3076
